TPU v7x, 256 devices: a whole 4x4x8 slice. The times are simulated.
256 devices in a mesh: seq: 64 (over x, y, z_lo), head: 4 (over z_hi, core).
Axes of the slice: x: 4, y: 4, z: 8 (z_hi: 2, z_lo: 4; z = z_hi * 4 + z_lo), core: 2. Of those that a mesh axis runs over, the one named last changes fastest.
Arguments:
- normed_input: bfloat16 [8192, 2304], P('seq'), may hold values from -16 to 16
- stored_queries: bfloat16 [8192, 2048], P('seq', 'head'), may hold values from -50 to 50
- stored_keys: bfloat16 [8192, 1024], P('seq', 'head'), may hold values from -4 to 4
- stored_values: bfloat16 [8192, 1024], P('seq', 'head'), may hold values from -6 to 6
- query_weight: bfloat16 [2304, 2048], P(None, 'head'), may hold values from -0.125 to 0.125
- key_matrix: bfloat16 [2304, 1024], P(None, 'head'), may hold values from -0.125 to 0.125
- value_matrix: bfloat16 [2304, 1024], P(None, 'head'), may hold values from -0.125 to 0.125
- output_weight: bfloat16 [2048, 2304], P('head'), may hold values from -0.125 to 0.125
- out_cotangent: bfloat16 [8192, 2304], P('seq'), may hold values from -128 to 128
Outputs:
- grad_input: bfloat16 [8192, 2304], P('seq', 'head')
- grad_wvalue: float32 [2304, 1024], P('seq', 'head')
- grad_woutput: float32 [2048, 2304], P('head', 'seq')
All inputs are finite; a program needn't handle non-finite values.
Results may differ from a plain program's by a relative error of at most 0.033.
Values may be sent and summed in bfloat16 or wider, within the bound.
A program may use at most 128 MiB of HBM per device.

v0:
```python
import jax
import jax.numpy as jnp
from jax import lax
from jax.sharding import PartitionSpec as P

HEAD_SIZE = 128
WINDOW_LENGTH = 4096
QUERIES_PER_KEY = 2


logit_scale = 1.0 / 12.0


def passed_along(value, axis, steps):
    count = lax.axis_size(axis)
    leading, last = (max(0, -steps), min(count, count - steps))
    return lax.ppermute(value, axis, [(source, source + steps) for source in range(leading, last)])


def local(
    normed_input,
    stored_queries,
    stored_keys,
    stored_values,
    query_weight,
    key_matrix,
    value_matrix,
    output_weight,
    out_cotangent,
):
    tok_rows = normed_input.shape[0]
    blocks_seq = lax.axis_size("seq")
    seq_place = lax.axis_index("seq")
    reach_blocks = min(WINDOW_LENGTH // tok_rows, blocks_seq - 1)
    kv_heads = stored_keys.shape[1] // HEAD_SIZE
    output_gradient = jnp.dot(
        out_cotangent, output_weight.T, preferred_element_type=jnp.float32
    ).astype(jnp.bfloat16)
    pieces = [
        passed_along((stored_keys, stored_values), "seq", distance)
        for distance in range(reach_blocks, 0, -1)
    ]
    pieces = pieces + [(stored_keys, stored_values)]
    key_window = jnp.concatenate([piece[0] for piece in pieces], axis=0)
    value_window = jnp.concatenate([piece[1] for piece in pieces], axis=0)
    key_span = key_window.shape[0]
    query_pos = seq_place * tok_rows + jnp.arange(tok_rows, dtype=jnp.int32)
    key_pos = (seq_place - reach_blocks) * tok_rows + jnp.arange(key_span, dtype=jnp.int32)
    pos_gap = query_pos[:, None] - key_pos[None, :]
    allowed = (pos_gap >= 0) & (pos_gap < WINDOW_LENGTH) & (key_pos >= 0)[None, :]
    allowed_rows = jnp.tile(allowed, (QUERIES_PER_KEY, 1))
    query_stack = (
        stored_queries.reshape(tok_rows, kv_heads, QUERIES_PER_KEY, HEAD_SIZE)
        .transpose(1, 2, 0, 3)
        .reshape(kv_heads, QUERIES_PER_KEY * tok_rows, HEAD_SIZE)
    )
    grad_stack = (
        output_gradient.reshape(tok_rows, kv_heads, QUERIES_PER_KEY, HEAD_SIZE)
        .transpose(1, 2, 0, 3)
        .reshape(kv_heads, QUERIES_PER_KEY * tok_rows, HEAD_SIZE)
    )
    key_stack = key_window.reshape(key_span, kv_heads, HEAD_SIZE).transpose(1, 0, 2)
    value_stack = value_window.reshape(key_span, kv_heads, HEAD_SIZE).transpose(1, 0, 2)

    def per_head(head_items):
        query_head, key_head, value_head, grad_head = head_items
        attention_logits = logit_scale * jnp.dot(
            query_head, key_head.T, preferred_element_type=jnp.float32
        )
        masked = jnp.where(allowed_rows, attention_logits, -jnp.inf)
        row_top = jnp.max(masked, axis=1, keepdims=True)
        exp_scores = jnp.exp(masked - row_top)
        attn_prob = exp_scores / jnp.sum(exp_scores, axis=1, keepdims=True)
        probability_halfwidth = attn_prob.astype(jnp.bfloat16)
        attn_head = jnp.dot(
            probability_halfwidth, value_head, preferred_element_type=jnp.float32
        ).astype(jnp.bfloat16)
        row_delta = jnp.sum(
            grad_head.astype(jnp.float32) * attn_head.astype(jnp.float32), axis=1, keepdims=True
        )
        probability_gradient = jnp.dot(grad_head, value_head.T, preferred_element_type=jnp.float32)
        score_gradient = (attn_prob * (probability_gradient - row_delta)).astype(jnp.bfloat16)
        qgrad_head = (
            logit_scale * jnp.dot(score_gradient, key_head, preferred_element_type=jnp.float32)
        ).astype(jnp.bfloat16)
        key_partial = logit_scale * jnp.dot(
            score_gradient.T, query_head, preferred_element_type=jnp.float32
        )
        value_partial = jnp.dot(
            probability_halfwidth.T, grad_head, preferred_element_type=jnp.float32
        )
        return (attn_head, qgrad_head, key_partial, value_partial)

    attn_all, qgrad_all, key_all, value_all = lax.map(
        per_head, (query_stack, key_stack, value_stack, grad_stack)
    )
    attention_output = (
        attn_all.reshape(kv_heads, QUERIES_PER_KEY, tok_rows, HEAD_SIZE)
        .transpose(2, 0, 1, 3)
        .reshape(tok_rows, kv_heads * QUERIES_PER_KEY * HEAD_SIZE)
    )
    query_gradient = (
        qgrad_all.reshape(kv_heads, QUERIES_PER_KEY, tok_rows, HEAD_SIZE)
        .transpose(2, 0, 1, 3)
        .reshape(tok_rows, kv_heads * QUERIES_PER_KEY * HEAD_SIZE)
    )
    key_terms = key_all.transpose(1, 0, 2).reshape(key_span, kv_heads * HEAD_SIZE)
    value_terms = value_all.transpose(1, 0, 2).reshape(key_span, kv_heads * HEAD_SIZE)

    def take_slot(terms, slot_index):
        return terms[slot_index * tok_rows : (slot_index + 1) * tok_rows]

    key_sum = take_slot(key_terms, reach_blocks)
    value_sum = take_slot(value_terms, reach_blocks)
    for distance in range(1, reach_blocks + 1):
        received = passed_along(
            (
                take_slot(key_terms, reach_blocks - distance),
                take_slot(value_terms, reach_blocks - distance),
            ),
            "seq",
            -distance,
        )
        key_sum = key_sum + received[0]
        value_sum = value_sum + received[1]
    grad_key = key_sum.astype(jnp.bfloat16)
    grad_value = value_sum.astype(jnp.bfloat16)
    input_terms = jnp.dot(query_gradient, query_weight.T, preferred_element_type=jnp.float32)
    input_terms = input_terms + jnp.dot(grad_key, key_matrix.T, preferred_element_type=jnp.float32)
    input_terms = input_terms + jnp.dot(
        grad_value, value_matrix.T, preferred_element_type=jnp.float32
    )
    grad_input = lax.psum_scatter(input_terms, "head", scatter_dimension=1, tiled=True).astype(
        jnp.bfloat16
    )
    value_cols = grad_value.shape[1]
    input_cols = normed_input.T
    cot_cols = out_cotangent.T
    gathered = lax.psum_scatter(
        jnp.concatenate(
            [
                jnp.dot(input_cols, grad_value, preferred_element_type=jnp.float32),
                jnp.dot(cot_cols, attention_output, preferred_element_type=jnp.float32),
            ],
            axis=1,
        ),
        "seq",
        scatter_dimension=0,
        tiled=True,
    )
    grad_wvalue = gathered[:, :value_cols]
    grad_woutput = gathered[:, value_cols:].T
    return (grad_input, grad_wvalue, grad_woutput)


def solution(mesh):
    placed = (
        P("seq", None),
        P("seq", "head"),
        P("seq", "head"),
        P("seq", "head"),
        P(None, "head"),
        P(None, "head"),
        P(None, "head"),
        P("head", None),
        P("seq", None),
    )
    return jax.shard_map(
        local,
        mesh=mesh,
        in_specs=placed,
        out_specs=(P("seq", "head"), P("seq", "head"), P("head", "seq")),
        check_vma=False,
    )
```

profile of v0, /device:TPU:128, one launch (start us, length us, event | category | flops | bytes accessed | tf_op | source)
XLA Modules:
  0.0 1823.7 jit_solution(17162068344724542063)
XLA Ops:
  463.1 13.3 collective-permute-start.63
  479.5 38.5 %while.17 = (s32[]{:T(128)}, bf16[2,256,128]{2,1,0:T(8,128)(2,1)S(1)}, bf16[2,256,128]{2,1,0:T(8,128)(2,1)}, f32[2,4224,128]{1,2,0:T(8,128)}, f32[2,4224,128]{1,...) while((s32[]{:T(128)}, ...), condition=%wide.region_4.5_spmd.clone, body=%wide.region_0.4_spmd.clone.sunk | while | flops 1679015168 | bytes 113738536 | solution.py:94
  579.3 19.4 %collective-permute-start.100 = (f32[128,256]{0,1:T(8,128)S(1)}, f32[128,256]{0,1:T(8,128)S(1)}, u32[]{:S(2)}, u32[]{:S(2)}) collective-permute-start(f32[128,256]{0,1:T(8,128)S(1)} %bitcast.349), channel_id=1, source_target_pairs={{20,0},{24,4},{28,8},{32,12},{36,16},{40,20},{44,24},{48,28},{52,3... | collective-permute-start | bytes 393224 | tf_op jit(solution)/shard_map/ppermute | solution.py:17
  599.2 13.2 collective-permute-start.101
  612.3 13.1 collective-permute-start.102
  625.5 13.1 collective-permute-start.103
  696.6 20.9 %collective-permute-start.64 = (f32[128,256]{0,1:T(8,128)S(1)}, f32[128,256]{0,1:T(8,128)S(1)}, u32[]{:S(2)}, u32[]{:S(2)}) collective-permute-start(f32[128,256]{0,1:T(8,128)S(1)} %bitcast.362), channel_id=1, source_target_pairs={{4,0},{8,4},{12,8},{16,12},{20,16},{24,20},{28,24},{32,28},{36,32}... | collective-permute-start | bytes 393224 | tf_op jit(solution)/shard_map/ppermute | solution.py:17
  717.5 13.1 collective-permute-start.65
  730.6 13.1 collective-permute-start.66
  743.8 13.1 collective-permute-start.67
  756.9 13.1 collective-permute-start.68
  770.1 13.3 collective-permute-start.69
  783.3 13.3 collective-permute-start.70
  796.6 13.3 collective-permute-start.71
  809.9 13.5 collective-permute-start.72
  824.5 13.5 collective-permute-start.73
  838.0 13.1 collective-permute-start.74
  851.2 13.1 collective-permute-start.75
  864.3 13.1 collective-permute-start.76
  877.4 13.1 collective-permute-start.77
  891.5 13.4 collective-permute-start.104
  904.9 13.1 collective-permute-start.105
  918.0 13.1 collective-permute-start.106
  931.2 13.1 collective-permute-start.107
  944.3 13.1 collective-permute-start.108
  959.9 13.3 collective-permute-start.109
  973.2 13.1 collective-permute-start.96
  986.3 13.1 collective-permute-start.97
  999.5 13.1 collective-permute-start.98
  1012.6 13.1 collective-permute-start.99
  1041.8 31.3 %reduce-scatter.3.cloned.1.call-done = f32[128,576]{0,1:T(8,128)} async-done(((f32[128,2304]{0,1:T(8,128)}), f32[128,576]{0,1:T(8,128)}) %reduce-scatter.3.cloned.1.call-update) | async-done | bytes 294928 | tf_op jit(solution)/shard_map/reduce_scatter | solution.py:133
  1074.8 737.8 %all-reduce.3.cloned.1.call-done = f32[2304,768]{0,1:T(8,128)} async-done(((f32[2304,768]{0,1:T(8,128)}), f32[2304,768]{0,1:T(8,128)}) %all-reduce.3.cloned.1.call-update) | async-done | bytes 7077904
  (538 shorter events, 638.7 us)
Async XLA Ops:
  8.0 1065.1 %reduce-scatter.3.cloned.1.call-start = ((), (), s32[]{:S(2)}) async-start(), calls=%async_computation.1 | async-start | bytes 1474560 | tf_op jit(solution)/shard_map/reduce_scatter | solution.py:133
  88.2 65.8 %collective-permute-start.20 = (bf16[128,256]{0,1:T(8,128)(2,1)S(1)}, bf16[128,256]{0,1:T(8,128)(2,1)S(1)}, u32[]{:S(2)}, u32[]{:S(2)}) collective-permute-start(bf16[128,256]{0,1:T(8,128)(2,1)S(1)} %copy.171), channel_id=1, source_target_pairs={{0,48},{4,52},{8,56},{12,60},{16,64},{20,68},{24,72},{28,76},{32,8... | collective-permute-start | bytes 196616 | tf_op jit(solution)/shard_map/ppermute | solution.py:17
  114.5 65.8 %collective-permute-start.22 = (bf16[128,256]{0,1:T(8,128)(2,1)S(1)}, bf16[128,256]{0,1:T(8,128)(2,1)S(1)}, u32[]{:S(2)}, u32[]{:S(2)}) collective-permute-start(bf16[128,256]{0,1:T(8,128)(2,1)S(1)} %copy.171), channel_id=1, source_target_pairs={{0,40},{4,44},{8,48},{12,52},{16,56},{20,60},{24,64},{28,68},{32,7... | collective-permute-start | bytes 196616 | tf_op jit(solution)/shard_map/ppermute | solution.py:17
  140.8 65.8 %collective-permute-start.24 = (bf16[128,256]{0,1:T(8,128)(2,1)S(1)}, bf16[128,256]{0,1:T(8,128)(2,1)S(1)}, u32[]{:S(2)}, u32[]{:S(2)}) collective-permute-start(bf16[128,256]{0,1:T(8,128)(2,1)S(1)} %copy.171), channel_id=1, source_target_pairs={{0,32},{4,36},{8,40},{12,44},{16,48},{20,52},{24,56},{28,60},{32,6... | collective-permute-start | bytes 196616 | tf_op jit(solution)/shard_map/ppermute | solution.py:17
  154.0 65.8 %collective-permute-start.25 = (bf16[128,256]{0,1:T(8,128)(2,1)S(1)}, bf16[128,256]{0,1:T(8,128)(2,1)S(1)}, u32[]{:S(2)}, u32[]{:S(2)}) collective-permute-start(bf16[128,256]{0,1:T(8,128)(2,1)S(1)} %copy.171), channel_id=1, source_target_pairs={{0,28},{4,32},{8,36},{12,40},{16,44},{20,48},{24,52},{28,56},{32,6... | collective-permute-start | bytes 196616 | tf_op jit(solution)/shard_map/ppermute | solution.py:17
  167.2 65.8 %collective-permute-start.26 = (bf16[128,256]{0,1:T(8,128)(2,1)S(1)}, bf16[128,256]{0,1:T(8,128)(2,1)S(1)}, u32[]{:S(2)}, u32[]{:S(2)}) collective-permute-start(bf16[128,256]{0,1:T(8,128)(2,1)S(1)} %copy.171), channel_id=1, source_target_pairs={{0,24},{4,28},{8,32},{12,36},{16,40},{20,44},{24,48},{28,52},{32,5... | collective-permute-start | bytes 196616 | tf_op jit(solution)/shard_map/ppermute | solution.py:17
  180.3 65.8 %collective-permute-start.27 = (bf16[128,256]{0,1:T(8,128)(2,1)S(1)}, bf16[128,256]{0,1:T(8,128)(2,1)S(1)}, u32[]{:S(2)}, u32[]{:S(2)}) collective-permute-start(bf16[128,256]{0,1:T(8,128)(2,1)S(1)} %copy.171), channel_id=1, source_target_pairs={{0,20},{4,24},{8,28},{12,32},{16,36},{20,40},{24,44},{28,48},{32,5... | collective-permute-start | bytes 196616 | tf_op jit(solution)/shard_map/ppermute | solution.py:17
  305.1 65.8 %collective-permute-start.51 = (bf16[128,256]{0,1:T(8,128)(2,1)S(1)}, bf16[128,256]{0,1:T(8,128)(2,1)S(1)}, u32[]{:S(2)}, u32[]{:S(2)}) collective-permute-start(bf16[128,256]{0,1:T(8,128)(2,1)S(1)} %copy.204), channel_id=1, source_target_pairs={{0,52},{4,56},{8,60},{12,64},{16,68},{20,72},{24,76},{28,80},{32,8... | collective-permute-start | bytes 196616 | tf_op jit(solution)/shard_map/ppermute | solution.py:17
  318.3 65.8 %collective-permute-start.52 = (bf16[128,256]{0,1:T(8,128)(2,1)S(1)}, bf16[128,256]{0,1:T(8,128)(2,1)S(1)}, u32[]{:S(2)}, u32[]{:S(2)}) collective-permute-start(bf16[128,256]{0,1:T(8,128)(2,1)S(1)} %copy.204), channel_id=1, source_target_pairs={{0,48},{4,52},{8,56},{12,60},{16,64},{20,68},{24,72},{28,76},{32,8... | collective-permute-start | bytes 196616 | tf_op jit(solution)/shard_map/ppermute | solution.py:17
  410.4 66.0 %collective-permute-start.59 = (bf16[128,256]{0,1:T(8,128)(2,1)S(1)}, bf16[128,256]{0,1:T(8,128)(2,1)S(1)}, u32[]{:S(2)}, u32[]{:S(2)}) collective-permute-start(bf16[128,256]{0,1:T(8,128)(2,1)S(1)} %copy.204), channel_id=1, source_target_pairs={{0,20},{4,24},{8,28},{12,32},{16,36},{20,40},{24,44},{28,48},{32,5... | collective-permute-start | bytes 196616 | tf_op jit(solution)/shard_map/ppermute | solution.py:17
  688.0 68.9 %collective-permute-start.95 = (f32[128,256]{0,1:T(8,128)S(1)}, f32[128,256]{0,1:T(8,128)S(1)}, u32[]{:S(2)}, u32[]{:S(2)}) collective-permute-start(f32[128,256]{0,1:T(8,128)S(1)} %bitcast.318), channel_id=1, source_target_pairs={{128,0},{132,4},{136,8},{140,12},{144,16},{148,20},{152,24},{156,2... | collective-permute-start | bytes 393224 | tf_op jit(solution)/shard_map/ppermute | solution.py:17
  696.6 73.5 %collective-permute-start.64 = (f32[128,256]{0,1:T(8,128)S(1)}, f32[128,256]{0,1:T(8,128)S(1)}, u32[]{:S(2)}, u32[]{:S(2)}) collective-permute-start(f32[128,256]{0,1:T(8,128)S(1)} %bitcast.362), channel_id=1, source_target_pairs={{4,0},{8,4},{12,8},{16,12},{20,16},{24,20},{28,24},{32,28},{36,32}... | collective-permute-start | bytes 393224 | tf_op jit(solution)/shard_map/ppermute | solution.py:17
  717.5 65.9 %collective-permute-start.65 = (f32[128,256]{0,1:T(8,128)S(1)}, f32[128,256]{0,1:T(8,128)S(1)}, u32[]{:S(2)}, u32[]{:S(2)}) collective-permute-start(f32[128,256]{0,1:T(8,128)S(1)} %bitcast.360), channel_id=1, source_target_pairs={{8,0},{12,4},{16,8},{20,12},{24,16},{28,20},{32,24},{36,28},{40,32... | collective-permute-start | bytes 393224 | tf_op jit(solution)/shard_map/ppermute | solution.py:17
  730.6 66.0 %collective-permute-start.66 = (f32[128,256]{0,1:T(8,128)S(1)}, f32[128,256]{0,1:T(8,128)S(1)}, u32[]{:S(2)}, u32[]{:S(2)}) collective-permute-start(f32[128,256]{0,1:T(8,128)S(1)} %bitcast.358), channel_id=1, source_target_pairs={{12,0},{16,4},{20,8},{24,12},{28,16},{32,20},{36,24},{40,28},{44,3... | collective-permute-start | bytes 393224 | tf_op jit(solution)/shard_map/ppermute | solution.py:17
  743.8 66.1 %collective-permute-start.67 = (f32[128,256]{0,1:T(8,128)S(1)}, f32[128,256]{0,1:T(8,128)S(1)}, u32[]{:S(2)}, u32[]{:S(2)}) collective-permute-start(f32[128,256]{0,1:T(8,128)S(1)} %bitcast.355), channel_id=1, source_target_pairs={{16,0},{20,4},{24,8},{28,12},{32,16},{36,20},{40,24},{44,28},{48,3... | collective-permute-start | bytes 393224 | tf_op jit(solution)/shard_map/ppermute | solution.py:17
  756.9 67.6 %collective-permute-start.68 = (f32[128,256]{0,1:T(8,128)}, f32[128,256]{0,1:T(8,128)}, u32[]{:S(2)}, u32[]{:S(2)}) collective-permute-start(f32[128,256]{0,1:T(8,128)} %bitcast.16), channel_id=1, source_target_pairs={{20,0},{24,4},{28,8},{32,12},{36,16},{40,20},{44,24},{48,28},{52,3... | collective-permute-start | bytes 393224 | tf_op jit(solution)/shard_map/ppermute | solution.py:17
  770.1 68.0 %collective-permute-start.69 = (f32[128,256]{0,1:T(8,128)}, f32[128,256]{0,1:T(8,128)}, u32[]{:S(2)}, u32[]{:S(2)}) collective-permute-start(f32[128,256]{0,1:T(8,128)} %bitcast.17), channel_id=1, source_target_pairs={{24,0},{28,4},{32,8},{36,12},{40,16},{44,20},{48,24},{52,28},{56,3... | collective-permute-start | bytes 393224 | tf_op jit(solution)/shard_map/ppermute | solution.py:17
  783.3 67.8 %collective-permute-start.70 = (f32[128,256]{0,1:T(8,128)}, f32[128,256]{0,1:T(8,128)}, u32[]{:S(2)}, u32[]{:S(2)}) collective-permute-start(f32[128,256]{0,1:T(8,128)} %bitcast.18), channel_id=1, source_target_pairs={{28,0},{32,4},{36,8},{40,12},{44,16},{48,20},{52,24},{56,28},{60,3... | collective-permute-start | bytes 393224 | tf_op jit(solution)/shard_map/ppermute | solution.py:17
  796.6 67.7 %collective-permute-start.71 = (f32[128,256]{0,1:T(8,128)}, f32[128,256]{0,1:T(8,128)}, u32[]{:S(2)}, u32[]{:S(2)}) collective-permute-start(f32[128,256]{0,1:T(8,128)} %bitcast.19), channel_id=1, source_target_pairs={{32,0},{36,4},{40,8},{44,12},{48,16},{52,20},{56,24},{60,28},{64,3... | collective-permute-start | bytes 393224 | tf_op jit(solution)/shard_map/ppermute | solution.py:17
  809.9 67.6 %collective-permute-start.72 = (f32[128,256]{0,1:T(8,128)}, f32[128,256]{0,1:T(8,128)}, u32[]{:S(2)}, u32[]{:S(2)}) collective-permute-start(f32[128,256]{0,1:T(8,128)} %bitcast.20), channel_id=1, source_target_pairs={{36,0},{40,4},{44,8},{48,12},{52,16},{56,20},{60,24},{64,28},{68,3... | collective-permute-start | bytes 393224 | tf_op jit(solution)/shard_map/ppermute | solution.py:17
  824.5 67.0 %collective-permute-start.73 = (f32[128,256]{0,1:T(8,128)}, f32[128,256]{0,1:T(8,128)S(1)}, u32[]{:S(2)}, u32[]{:S(2)}) collective-permute-start(f32[128,256]{0,1:T(8,128)} %bitcast.340), channel_id=1, source_target_pairs={{40,0},{44,4},{48,8},{52,12},{56,16},{60,20},{64,24},{68,28},{72,3... | collective-permute-start | bytes 393224 | tf_op jit(solution)/shard_map/ppermute | solution.py:17
  838.0 66.9 %collective-permute-start.74 = (f32[128,256]{0,1:T(8,128)}, f32[128,256]{0,1:T(8,128)S(1)}, u32[]{:S(2)}, u32[]{:S(2)}) collective-permute-start(f32[128,256]{0,1:T(8,128)} %bitcast.337), channel_id=1, source_target_pairs={{44,0},{48,4},{52,8},{56,12},{60,16},{64,20},{68,24},{72,28},{76,3... | collective-permute-start | bytes 393224 | tf_op jit(solution)/shard_map/ppermute | solution.py:17
  851.2 66.9 %collective-permute-start.75 = (f32[128,256]{0,1:T(8,128)}, f32[128,256]{0,1:T(8,128)S(1)}, u32[]{:S(2)}, u32[]{:S(2)}) collective-permute-start(f32[128,256]{0,1:T(8,128)} %bitcast.334), channel_id=1, source_target_pairs={{48,0},{52,4},{56,8},{60,12},{64,16},{68,20},{72,24},{76,28},{80,3... | collective-permute-start | bytes 393224 | tf_op jit(solution)/shard_map/ppermute | solution.py:17
  864.3 66.9 %collective-permute-start.76 = (f32[128,256]{0,1:T(8,128)}, f32[128,256]{0,1:T(8,128)S(1)}, u32[]{:S(2)}, u32[]{:S(2)}) collective-permute-start(f32[128,256]{0,1:T(8,128)} %bitcast.331), channel_id=1, source_target_pairs={{52,0},{56,4},{60,8},{64,12},{68,16},{72,20},{76,24},{80,28},{84,3... | collective-permute-start | bytes 393224 | tf_op jit(solution)/shard_map/ppermute | solution.py:17
  877.4 66.9 %collective-permute-start.77 = (f32[128,256]{0,1:T(8,128)}, f32[128,256]{0,1:T(8,128)S(1)}, u32[]{:S(2)}, u32[]{:S(2)}) collective-permute-start(f32[128,256]{0,1:T(8,128)} %bitcast.329), channel_id=1, source_target_pairs={{56,0},{60,4},{64,8},{68,12},{72,16},{76,20},{80,24},{84,28},{88,3... | collective-permute-start | bytes 393224 | tf_op jit(solution)/shard_map/ppermute | solution.py:17
  891.5 68.4 %collective-permute-start.104 = (f32[128,256]{0,1:T(8,128)S(1)}, f32[128,256]{0,1:T(8,128)S(1)}, u32[]{:S(2)}, u32[]{:S(2)}) collective-permute-start(f32[128,256]{0,1:T(8,128)S(1)} %bitcast.317), channel_id=1, source_target_pairs={{36,0},{40,4},{44,8},{48,12},{52,16},{56,20},{60,24},{64,28},{68,3... | collective-permute-start | bytes 393224 | tf_op jit(solution)/shard_map/ppermute | solution.py:17
  904.9 68.3 %collective-permute-start.105 = (f32[128,256]{0,1:T(8,128)S(1)}, f32[128,256]{0,1:T(8,128)S(1)}, u32[]{:S(2)}, u32[]{:S(2)}) collective-permute-start(f32[128,256]{0,1:T(8,128)S(1)} %bitcast.316), channel_id=1, source_target_pairs={{40,0},{44,4},{48,8},{52,12},{56,16},{60,20},{64,24},{68,28},{72,3... | collective-permute-start | bytes 393224 | tf_op jit(solution)/shard_map/ppermute | solution.py:17
  918.0 68.3 %collective-permute-start.106 = (f32[128,256]{0,1:T(8,128)S(1)}, f32[128,256]{0,1:T(8,128)S(1)}, u32[]{:S(2)}, u32[]{:S(2)}) collective-permute-start(f32[128,256]{0,1:T(8,128)S(1)} %bitcast.315), channel_id=1, source_target_pairs={{44,0},{48,4},{52,8},{56,12},{60,16},{64,20},{68,24},{72,28},{76,3... | collective-permute-start | bytes 393224 | tf_op jit(solution)/shard_map/ppermute | solution.py:17
  931.2 68.3 %collective-permute-start.107 = (f32[128,256]{0,1:T(8,128)S(1)}, f32[128,256]{0,1:T(8,128)S(1)}, u32[]{:S(2)}, u32[]{:S(2)}) collective-permute-start(f32[128,256]{0,1:T(8,128)S(1)} %bitcast.314), channel_id=1, source_target_pairs={{48,0},{52,4},{56,8},{60,12},{64,16},{68,20},{72,24},{76,28},{80,3... | collective-permute-start | bytes 393224 | tf_op jit(solution)/shard_map/ppermute | solution.py:17
  944.3 68.3 %collective-permute-start.108 = (f32[128,256]{0,1:T(8,128)S(1)}, f32[128,256]{0,1:T(8,128)S(1)}, u32[]{:S(2)}, u32[]{:S(2)}) collective-permute-start(f32[128,256]{0,1:T(8,128)S(1)} %bitcast.313), channel_id=1, source_target_pairs={{52,0},{56,4},{60,8},{64,12},{68,16},{72,20},{76,24},{80,28},{84,3... | collective-permute-start | bytes 393224 | tf_op jit(solution)/shard_map/ppermute | solution.py:17
  959.9 66.4 %collective-permute-start.109 = (f32[128,256]{0,1:T(8,128)S(1)}, f32[128,256]{0,1:T(8,128)S(1)}, u32[]{:S(2)}, u32[]{:S(2)}) collective-permute-start(f32[128,256]{0,1:T(8,128)S(1)} %bitcast.312), channel_id=1, source_target_pairs={{56,0},{60,4},{64,8},{68,12},{72,16},{76,20},{80,24},{84,28},{88,3... | collective-permute-start | bytes 393224 | tf_op jit(solution)/shard_map/ppermute | solution.py:17
  1034.8 777.8 %all-reduce.3.cloned.1.call-start = ((), (), s32[]{:S(2)}) async-start(), calls=%async_computation.2 | async-start | bytes 14155776
  (187 other events, 8911.7 us)
Sparse Core Ops, SparseCore 0:
  1034.9 38.1 reduce-scatter.2
Sparse Core Ops, SparseCore 1:
  1040.0 772.5 all-reduce.2
where the time goes:
time: 1830 us; the launch traced here: 1820 us
  starting transfers between devices  886 us (48%)
  waiting for transfers between devices  843 us (46%)
  local copies, waits for them, and re-layouts  39.4 us (2%)
  matrix products  25.4 us (1%)
  between operations  19 us (1%)
    ppermute x128, starting transfers between devices, passed_along(): lax.ppermute(value, axis, [(source, source + steps) for source in range(l...  886 us
    unnamed x3, waiting for transfers between devices  738 us
    ppermute x128, waiting for transfers between devices, passed_along(): lax.ppermute(value, axis, [(source, source + steps) for source in range(l...  73.6 us
  transfers between devices with their start and end apart: 130, of which 23 were waited for; matrix products, arithmetic and copies ran while one was open for 1% of the time, Pallas kernels for 0%

commit v1 on v0

v1 whole, which is shorter than its diff:
```python
import functools
import math

import jax
import jax.numpy as jnp
from jax import lax
from jax.experimental import pallas as pl
from jax.experimental.pallas import tpu as pltpu
from jax.sharding import PartitionSpec as P

MESH = pl.DeviceIdType.MESH
F32 = jnp.float32
BF16 = jnp.bfloat16
LOGIT_SCALE = 1.0 / 12.0
EXP2_SCALE = LOGIT_SCALE * math.log2(math.e)
NEG = -1e30
T = 128
D = 128
SLOTS = 9
ROWS = 1024
WIN = 640
COLS = 576
SPLIT = 5
KEYS = 256
NT = (((1,), (1,)), ((), ()))


def dot(a, b):
    return jnp.dot(a, b, preferred_element_type=F32)


def place():
    i = lax.axis_index("seq")
    h = lax.axis_index("head")
    x = lax.div(i, 16)
    y = lax.rem(lax.div(i, 4), 4)
    z = lax.rem(i, 4)
    return i, h, x, y, z


def layer_kernel(
    x_hbm, q_hbm, k_hbm, v_hbm, wq_hbm, wk_hbm, wv_hbm, wo_hbm, cot_hbm,
    gi_o, gwv_o, gwo_o,
    attn_o, gq_o, gk_o, gv_o, wq, wk, wv, win, winT, ag, gvg, po, pv, yo, yv, zso, zsv, zpo, zpv, zio, ziv, tb, hin,
    kv, qg, dog, og, cot, wo, q2, do2, qT, doT, sbuf, dpbuf, pb_s, ds_s, ms, st, st_in, fin,
    oT, dqT, osend, oin, dqsend, dqin, dkv, rbuf, csend, cin, finkv, pin,
    lsem, pair_s, pair_r, q_s, q_r, do_s, do_r, kvx_s, kvy_s, kv_r, st_s, st_r, o_s, o_r, dq_s, dq_r,
    rb_s, rb_r, c_s, c_r, f_s, f_r,
    w_s, w_r, ag_s, ag_r, gg_s, gg_r, yo_s, yo_r, yv_s, yv_r, zo_s, zo_r, zv_s, zv_r, h_s, h_r,
):
    i, h, x, y, z = place()
    e, f = lax.rem(z, 2), lax.div(z, 2)
    S = x * 4 + y

    def dev(x_, y_, z_):
        return (x_ * 16 + y_ * 4 + z_, h)

    def wrap(a):
        return lax.rem(a + 4, 4)

    def remote(src, dst, s, r, to):
        return pltpu.make_async_remote_copy(
            src_ref=src, dst_ref=dst, send_sem=s, recv_sem=r, device_id=to, device_id_type=MESH
        )

    erow = pl.multiple_of(e * T, T)
    prow = pl.multiple_of((1 - e) * T, T)
    ecol2 = pl.multiple_of(e * 256, 256)
    c_wo = pltpu.make_async_copy(wo_hbm, wo, lsem.at[0])
    c_cot = pltpu.make_async_copy(cot_hbm, cot, lsem.at[1])
    c_k = pltpu.make_async_copy(k_hbm.at[:, pl.ds(erow, D)], kv.at[0, 0, pl.ds(erow, T), :], lsem.at[2])
    c_v = pltpu.make_async_copy(v_hbm.at[:, pl.ds(erow, D)], kv.at[0, 1, pl.ds(erow, T), :], lsem.at[3])
    c_q = pltpu.make_async_copy(q_hbm.at[:, pl.ds(ecol2, 256)], qg.at[z], lsem.at[4])
    for c in (c_wo, c_cot, c_k, c_v, c_q):
        c.start()

    def window(xt):
        return pl.ds(pl.multiple_of(lax.div(9 * xt, 2) * 128, 128), WIN)

    c_win = [
        pltpu.make_async_copy(src.at[:, window(x)], win.at[n, x], lsem.at[5 + n]) for n, src in ((0, x_hbm), (1, cot_hbm))
    ]
    c_w = [pltpu.make_async_copy(src, dst, lsem.at[7 + n]) for n, (src, dst) in enumerate(((wq_hbm, wq), (wk_hbm, wk), (wv_hbm, wv)))]

    bar = pltpu.get_barrier_semaphore()
    for r in (1, 2, 3):
        for to in (dev(x, y, wrap(z + r)), dev(x, wrap(y + r), z), dev(wrap(x + r), y, z)):
            pl.semaphore_signal(bar, inc=1, device_id=to, device_id_type=MESH)
    hc = h + 1 - 2 * lax.rem(h, 2)
    hz = lax.rem(h + 2, 4)
    for to in ((i, hc), (i, hz)):
        pl.semaphore_signal(bar, inc=1, device_id=to, device_id_type=MESH)
    pl.semaphore_wait(bar, 11)

    zp = z + 1 - 2 * e
    pair = [
        remote(src.at[:, pl.ds(prow, D)], kv.at[0, n, pl.ds(erow, T), :], pair_s.at[n], pair_r.at[n], dev(x, y, zp))
        for n, src in ((0, k_hbm), (1, v_hbm))
    ]
    for c in pair:
        c.start()

    def gathered(src_of, buf, s, r_):
        copies = []
        for r in (1, 2, 3):
            zt = wrap(z + r)
            copies.append(remote(src_of(zt), buf.at[z], s.at[r - 1], r_.at[r - 1], dev(x, y, zt)))
        return copies

    qcopies = gathered(
        lambda zt: q_hbm.at[:, pl.ds(pl.multiple_of(lax.rem(zt, 2) * 256, 256), 256)], qg, q_s, q_r
    )
    for c in qcopies:
        c.start()

    c_wo.wait()
    c_cot.wait()
    grad = lax.dot_general(cot[...], wo[...], NT, preferred_element_type=F32).astype(BF16)
    og[0] = grad[:, :256]
    og[1] = grad[:, 256:]
    docopies = gathered(lambda zt: og.at[lax.rem(zt, 2)], dog, do_s, do_r)
    for c in docopies:
        c.start()
    dog[z] = og[e]

    c_k.wait()
    c_v.wait()
    for c in pair:
        c.wait_recv()

    def fwd_x(src, dst):
        return remote(kv.at[src], kv.at[dst], kvx_s.at[dst // 8], kv_r.at[dst], dev(wrap(x + 1), y, z))

    def fwd_y(r, kind):
        yt = wrap(y + r)
        up = yt > y
        if kind == 0:
            src, dst = 4, 4 + yt - y
        else:
            src, dst = jnp.where(up, 0, 8), jnp.where(up, yt - y, 8 + yt - y)
        return remote(kv.at[src], kv.at[dst], kvy_s.at[kind * 3 + r - 1], kv_r.at[dst], dev(x, yt, z))

    @pl.when(x < 3)
    def _():
        fwd_x(0, 4).start()

    for r in (1, 2, 3):
        @pl.when(y + r < 4)
        def _():
            fwd_y(r, 1).start()

    def recv_slot(d):
        remote(kv.at[d], kv.at[d], kvx_s.at[0], kv_r.at[d], dev(wrap(x + 1), y, z)).wait_recv()

    @pl.when(x >= 1)
    def _():
        recv_slot(4)
        for r in (1, 2, 3):
            fwd_y(r, 0).start()

    @pl.when((x >= 1) & (x < 3))
    def _():
        fwd_x(4, 8).start()

    wcopies = []
    for r in (1, 2, 3):
        xt = wrap(x + r)
        for n, src in ((0, x_hbm), (1, cot_hbm)):
            wcopies.append(
                remote(src.at[:, window(xt)], win.at[n, x], w_s.at[n, r - 1], w_r.at[n, r - 1], dev(xt, y, z))
            )
    for c in wcopies + c_win + c_w:
        c.start()

    c_q.wait()
    for r in (1, 2, 3):
        qcopies[r - 1].wait_recv()
    for r in (1, 2, 3):
        docopies[r - 1].wait_recv()

    @pl.loop(0, 4)
    def _(zz):
        for j in range(2):
            rows = pl.ds(pl.multiple_of(j * 512 + zz * T, T), T)
            qb = qg[zz, :, j * D : (j + 1) * D]
            q2[rows, :] = qb
            qT[:, rows] = qb.T
            db = dog[zz, :, j * D : (j + 1) * D]
            do2[rows, :] = db
            doT[:, rows] = db.T

    @pl.when(x >= 2)
    def _():
        recv_slot(8)
        for r in (1, 2, 3):
            @pl.when(y + r >= 4)
            def _():
                fwd_y(r, 1).start()

    st[...] = jnp.concatenate([jnp.full((1, ROWS), NEG, F32), jnp.zeros((7, ROWS), F32)], axis=0)
    oT[...] = jnp.zeros_like(oT)
    dqT[...] = jnp.zeros_like(dqT)

    def slot_of(kind, r):
        if kind == 0:
            return 4 + jnp.where(r <= y, r, r - 4)
        return jnp.where(r <= y, r, r + 4)

    @pl.loop(0, SLOTS)
    def _(t):
        d = jnp.where(
            t < 2, t * 4, jnp.where(t == 8, 8, jnp.where(t < 5, slot_of(1, t - 1), slot_of(0, t - 4)))
        )

        @pl.when(S >= d)
        def _():
            @pl.when((t >= 2) & (t < 8))
            def _():
                recv_slot(d)

            kd = kv[d, 0]
            vd = kv[d, 1]
            vt = vd.T
            low = jnp.where(d == 0, 0, -100000)
            high = jnp.where(d == 8, 0, 100000)
            for c in range(4):
                cs = slice(c * 256, (c + 1) * 256)
                s = dot(kd, qT[:, cs])
                gap = (
                    lax.broadcasted_iota(jnp.int32, (KEYS, 256), 1)
                    - lax.broadcasted_iota(jnp.int32, (KEYS, 256), 0)
                    + ((c % 2) * 256 - f * 256)
                )
                s = jnp.where((gap >= low) & (gap < high), s, NEG)
                before = st[0:1, cs]
                top = jnp.maximum(before, jnp.max(s, axis=0, keepdims=True))
                p = jnp.exp2((s - top) * EXP2_SCALE)
                keep = jnp.exp2((before - top) * EXP2_SCALE)
                dp = dot(vd, doT[:, cs])
                st[0:1, cs] = top
                st[1:2, cs] = st[1:2, cs] * keep + jnp.sum(p, axis=0, keepdims=True)
                st[2:3, cs] = st[2:3, cs] * keep + jnp.sum(p * dp, axis=0, keepdims=True)
                ms[d, 0:1, cs] = top
                sbuf[d, :, cs] = p
                dpbuf[d, :, cs] = dp
                oT[:, cs] = oT[:, cs] * keep + dot(vt, p.astype(BF16))

    stat = remote(st, st_in, st_s, st_r, dev(x, y, wrap(z + 2)))
    stat.start()
    stat.wait()
    top = jnp.maximum(st[0:1, :], st_in[0:1, :])
    mine = jnp.exp2((st[0:1, :] - top) * EXP2_SCALE)
    other = jnp.exp2((st_in[0:1, :] - top) * EXP2_SCALE)
    inv = 1.0 / (st[1:2, :] * mine + st_in[1:2, :] * other)
    fin[0:1, :] = top
    fin[1:2, :] = inv
    fin[2:3, :] = (st[2:3, :] * mine + st_in[2:3, :] * other) * inv
    oT[...] = oT[...] * (mine * inv)

    def spread(srcT, factor, sendbuf, inbuf, s, r_):
        for j in range(2):
            for zz in range(4):
                piece = srcT[:, j * 512 + zz * T : j * 512 + (zz + 1) * T]
                sendbuf[zz, :, j * D : (j + 1) * D] = (piece * factor).T.astype(BF16)
        copies = []
        for r in (1, 2, 3):
            zt = wrap(z + r)
            copies.append(remote(sendbuf.at[zt], inbuf.at[z], s.at[r - 1], r_.at[r - 1], dev(x, y, zt)))
        for c in copies:
            c.start()
        inbuf[z] = sendbuf[z]
        return copies

    ocopies = spread(oT, 1.0, osend, oin, o_s, o_r)

    def grad_slot(d):
        w = jnp.exp2((ms[d, 0:1, :] - fin[0:1, :]) * EXP2_SCALE) * fin[1:2, :]
        kt = kv[d, 0].T
        for c in range(4):
            cs = slice(c * 256, (c + 1) * 256)
            p = sbuf[d, :, cs] * w[:, cs]
            pb_s[:, cs] = p.astype(BF16)
            ds = (p * (dpbuf[d, :, cs] - fin[2:3, cs])).astype(BF16)
            ds_s[:, cs] = ds
            dqT[:, cs] += dot(kt, ds)
        dkv[d, 0] = (LOGIT_SCALE * dot(ds_s[...], q2[...])).astype(BF16)
        dkv[d, 1] = dot(pb_s[...], do2[...]).astype(BF16)

    def back_y(kind, r):
        d = slot_of(kind, r)
        n = kind * 3 + r - 1
        return remote(dkv.at[d], rbuf.at[n], rb_s.at[n], rb_r.at[n], dev(x, wrap(y - r), z))

    def grad_step(t):
        d = jnp.where(
            t >= 6, 8 - (t - 6) * 4, jnp.where(t < 3, slot_of(0, t + 1), slot_of(1, t - 2))
        )

        @pl.when(S >= d)
        def _():
            grad_slot(d)

            @pl.when(t < 6)
            def _():
                r = lax.rem(t, 3) + 1
                remote(dkv.at[d], rbuf.at[t], rb_s.at[t], rb_r.at[t], dev(x, wrap(y - r), z)).start()

    pl.loop(0, SPLIT)(grad_step)

    def over_x(src, dst, s, r_):
        return [remote(src, dst, s.at[r - 1], r_.at[r - 1], dev(wrap(x + r), y, z)) for r in (1, 2, 3)]

    for c in ocopies:
        c.wait_recv()
    for n in range(2):
        attn_o[n] = (oin[n].astype(F32) + oin[n + 2].astype(F32)).astype(BF16)
    agcopies = over_x(attn_o, ag.at[:, x], ag_s, ag_r)
    for c in agcopies:
        c.start()
    ag[:, x] = attn_o[...]

    pl.loop(SPLIT, SLOTS)(grad_step)

    dqcopies = spread(dqT, LOGIT_SCALE, dqsend, dqin, dq_s, dq_r)

    def recv_back(n):
        remote(rbuf.at[n], rbuf.at[n], rb_s.at[n], rb_r.at[n], dev(x, wrap(y + 1), z)).wait_recv()

    chain8 = remote(csend.at[0], cin.at[0], c_s.at[0], c_r.at[0], dev(wrap(x - 1), y, z))
    chain4 = remote(csend.at[1], cin.at[1], c_s.at[1], c_r.at[1], dev(wrap(x - 1), y, z))

    for c in c_win:
        c.wait()
    for c in wcopies:
        c.wait_recv()

    @pl.loop(0, 4)
    def _(xx):
        for n in range(2):
            for b in range(WIN // 128):
                cols = slice(b * 128, (b + 1) * 128)
                winT[n, cols, pl.ds(pl.multiple_of(xx * T, T), T)] = win[n, xx, :, cols].T

    for r in (1, 2, 3):
        @pl.when((y + r < 4) | (x >= 2))
        def _():
            recv_back(3 + r - 1)

    @pl.when(x >= 2)
    def _():
        for n in range(2):
            acc = dkv[8, n].astype(F32)
            for r in (1, 2, 3):
                acc = acc + jnp.where(y + r >= 4, rbuf[3 + r - 1, n].astype(F32), 0.0)
            csend[0, n] = acc.astype(BF16)
        chain8.start()

    @pl.when(x >= 1)
    def _():
        for r in (1, 2, 3):
            recv_back(r - 1)

        @pl.when(x < 3)
        def _():
            chain8.wait_recv()

        for n in range(2):
            acc = dkv[4, n].astype(F32)
            for r in (1, 2, 3):
                acc = acc + rbuf[r - 1, n].astype(F32)
            acc = acc + jnp.where(x < 3, cin[0, n].astype(F32), 0.0)
            csend[1, n] = acc.astype(BF16)
        chain4.start()

    off = pl.multiple_of(64 * lax.rem(x, 2), 16)

    def over_y(src, buf, s, r_):
        copies = []
        for r in (1, 2, 3):
            yt = wrap(y + r)
            rows = pl.ds(pl.multiple_of(off + 144 * yt, 16), 144)
            copies.append(remote(src.at[rows, :], buf.at[r - 1], s.at[r - 1], r_.at[r - 1], dev(x, yt, z)))
        return copies

    for c in agcopies:
        c.wait_recv()
    for n in range(2):
        po[:, n * 256 : (n + 1) * 256] = dot(winT[1], ag[n].reshape(4 * T, 256)).astype(BF16)
    yocopies = over_y(po, yo, yo_s, yo_r)
    for c in yocopies:
        c.start()

    @pl.when(x < 3)
    def _():
        chain4.wait_recv()

    for n in range(2):
        acc = dkv[0, n].astype(F32)
        for r in (1, 2, 3):
            acc = acc + jnp.where(y + r < 4, rbuf[3 + r - 1, n].astype(F32), 0.0)
        acc = acc + jnp.where(x < 3, cin[1, n].astype(F32), 0.0)
        finkv[n] = acc.astype(BF16)

    swap = [
        remote(finkv.at[n, pl.ds(prow, T), :], pin.at[n], f_s.at[n], f_r.at[n], dev(x, y, zp)) for n in range(2)
    ]
    for c in swap:
        c.start()

    for c in dqcopies:
        c.wait_recv()
    for n in range(2):
        gq_o[n] = (dqin[n].astype(F32) + dqin[n + 2].astype(F32)).astype(BF16)
    for c in c_w:
        c.wait()
    for c in swap:
        c.wait_recv()
    for n, out in ((0, gk_o), (1, gv_o)):
        out[e] = finkv[n, pl.ds(erow, T), :]
        out[1 - e] = pin[n]
    ggcopies = over_x(gv_o, gvg.at[:, x], gg_s, gg_r)
    for c in ggcopies:
        c.start()
    gvg[:, x] = gv_o[...]

    def terms(hh):
        rows = pl.ds(pl.multiple_of(COLS * hh, 16), COLS)
        acc = jnp.zeros((T, COLS), F32)
        for n in range(2):
            acc = acc + lax.dot_general(gq_o[n], wq[rows, n * 256 : (n + 1) * 256], NT, preferred_element_type=F32)
            acc = acc + lax.dot_general(gk_o[n], wk[rows, n * D : (n + 1) * D], NT, preferred_element_type=F32)
            acc = acc + lax.dot_general(gv_o[n], wv[rows, n * D : (n + 1) * D], NT, preferred_element_type=F32)
        return acc

    hzc = lax.rem(hc + 2, 4)
    tb[0] = terms(hzc).astype(BF16)
    far = remote(tb.at[0], hin.at[0], h_s.at[0], h_r.at[0], (i, hc))
    far.start()
    mine_far = terms(hz)
    far.wait_recv()
    tb[1] = (mine_far + hin[0].astype(F32)).astype(BF16)
    across = remote(tb.at[1], hin.at[1], h_s.at[1], h_r.at[1], (i, hz))
    across.start()
    tb[2] = terms(hc).astype(BF16)
    near = remote(tb.at[2], hin.at[2], h_s.at[2], h_r.at[2], (i, hc))
    near.start()

    for c in ggcopies:
        c.wait_recv()
    for n in range(2):
        pv[:, n * D : (n + 1) * D] = dot(winT[0], gvg[n].reshape(4 * T, D)).astype(BF16)
    yvcopies = over_y(pv, yv, yv_s, yv_r)
    for c in yvcopies:
        c.start()

    def over_z(copies, own, buf, total_s, piece_s, in_s, s, r_):
        for c in copies:
            c.wait_recv()
        acc = own[pl.ds(pl.multiple_of(off + 144 * y, 16), 144), :].astype(F32)
        for r in range(3):
            acc = acc + buf[r].astype(F32)
        total_s[...] = acc
        for zz in range(4):
            piece_s[zz] = total_s[36 * zz : 36 * (zz + 1), :]
        out = []
        for r in (1, 2, 3):
            zt = wrap(z + r)
            out.append(remote(piece_s.at[zt], in_s.at[r - 1], s.at[r - 1], r_.at[r - 1], dev(x, y, zt)))
        for c in out:
            c.start()
        return out

    zocopies = over_z(yocopies, po, yo, zso, zpo, zio, zo_s, zo_r)
    mine_near = terms(h)
    zvcopies = over_z(yvcopies, pv, yv, zsv, zpv, ziv, zv_s, zv_r)

    for c in zocopies:
        c.wait_recv()
    acc = zpo[z]
    for r in range(3):
        acc = acc + zio[r]
    gwo_o[...] = acc
    near.wait_recv()
    across.wait_recv()
    gi_o[...] = (mine_near + hin[2].astype(F32) + hin[1].astype(F32)).astype(BF16)
    for c in zvcopies:
        c.wait_recv()
    acc = zpv[z]
    for r in range(3):
        acc = acc + ziv[r]
    gwv_o[...] = acc

    for c in (
        pair + qcopies + docopies + ocopies + dqcopies + swap + wcopies + agcopies + ggcopies
        + yocopies + yvcopies + zocopies + zvcopies + [far, across, near]
    ):
        c.wait_send()

    @pl.when(x < 3)
    def _():
        fwd_x(0, 4).wait_send()

    @pl.when((x >= 1) & (x < 3))
    def _():
        fwd_x(4, 8).wait_send()

    for r in (1, 2, 3):
        @pl.when((y + r < 4) | (x >= 2))
        def _():
            fwd_y(r, 1).wait_send()

        @pl.when(x >= 1)
        def _():
            fwd_y(r, 0).wait_send()
            back_y(0, r).wait_send()

        @pl.when((r <= y) | (x >= 2))
        def _():
            back_y(1, r).wait_send()

    @pl.when(x >= 2)
    def _():
        chain8.wait_send()

    @pl.when(x >= 1)
    def _():
        chain4.wait_send()


def layer(xn, q, k, v, wq, wk, wv, wo, cot):
    dma = pltpu.SemaphoreType.DMA
    vm = pltpu.VMEM
    return pl.pallas_call(
        layer_kernel,
        out_shape=(
            jax.ShapeDtypeStruct((T, COLS), BF16),
            jax.ShapeDtypeStruct((36, 256), F32),
            jax.ShapeDtypeStruct((36, 512), F32),
        ),
        in_specs=[pl.BlockSpec(memory_space=pl.ANY)] * 9,
        out_specs=tuple(pl.BlockSpec(memory_space=pltpu.VMEM) for _ in range(3)),
        scratch_shapes=[
            vm((2, T, 256), BF16),
            vm((2, T, 256), BF16),
            vm((2, T, D), BF16),
            vm((2, T, D), BF16),
            vm(wq.shape, BF16),
            vm(wk.shape, BF16),
            vm(wv.shape, BF16),
            vm((2, 4, T, WIN), BF16),
            vm((2, WIN, 4 * T), BF16),
            vm((2, 4, T, 256), BF16),
            vm((2, 4, T, D), BF16),
            vm((WIN, 512), BF16),
            vm((WIN, 256), BF16),
            vm((3, 144, 512), BF16),
            vm((3, 144, 256), BF16),
            vm((144, 512), F32),
            vm((144, 256), F32),
            vm((4, 36, 512), F32),
            vm((4, 36, 256), F32),
            vm((3, 36, 512), F32),
            vm((3, 36, 256), F32),
            vm((3, T, COLS), BF16),
            vm((3, T, COLS), BF16),
            vm((SLOTS, 2, KEYS, D), BF16),
            vm((4, T, 256), BF16),
            vm((4, T, 256), BF16),
            vm((2, T, 256), BF16),
            vm(cot.shape, BF16),
            vm(wo.shape, BF16),
            vm((ROWS, D), BF16),
            vm((ROWS, D), BF16),
            vm((D, ROWS), BF16),
            vm((D, ROWS), BF16),
            vm((SLOTS, KEYS, ROWS), F32),
            vm((SLOTS, KEYS, ROWS), F32),
            vm((KEYS, ROWS), BF16),
            vm((KEYS, ROWS), BF16),
            vm((SLOTS, 8, ROWS), F32),
            vm((8, ROWS), F32),
            vm((8, ROWS), F32),
            vm((8, ROWS), F32),
            vm((D, ROWS), F32),
            vm((D, ROWS), F32),
            vm((4, T, 256), BF16),
            vm((4, T, 256), BF16),
            vm((4, T, 256), BF16),
            vm((4, T, 256), BF16),
            vm((SLOTS, 2, KEYS, D), BF16),
            vm((6, 2, KEYS, D), BF16),
            vm((2, 2, KEYS, D), BF16),
            vm((2, 2, KEYS, D), BF16),
            vm((2, KEYS, D), BF16),
            vm((2, T, D), BF16),
            dma((10,)), dma((2,)), dma((2,)), dma((3,)), dma((3,)), dma((3,)), dma((3,)),
            dma((2,)), dma((6,)), dma((SLOTS,)), dma, dma, dma((3,)), dma((3,)), dma((3,)), dma((3,)),
            dma((6,)), dma((6,)), dma((2,)), dma((2,)), dma((2,)), dma((2,)),
            dma((2, 3)), dma((2, 3)), *([dma((3,))] * 14),
        ],
        compiler_params=pltpu.CompilerParams(
            collective_id=1, has_side_effects=True, vmem_limit_bytes=62 * 1024 * 1024
        ),
        name="layer",
    )(xn, q, k, v, wq, wk, wv, wo, cot)


def local(*args):
    grad_input, grad_wvalue, grad_woutput = layer(*args)
    return grad_input, grad_wvalue, grad_woutput.T


def solution(mesh):
    seq, both, cols, rows = P("seq", None), P("seq", "head"), P(None, "head"), P("head", None)
    return jax.shard_map(
        local,
        mesh=mesh,
        in_specs=(seq, both, both, both, cols, cols, cols, rows, seq),
        out_specs=(both, both, P("head", "seq")),
        check_vma=False,
    )
```

time: 1830 us -> 99.7 us (0.05)
  the two profiles are of different devices: /device:TPU:128 before, /device:TPU:1 now
where the time goes in v1:
time: 99.7 us; the launch traced here: 99.5 us
  Pallas kernels  94.2 us (94%)
  local copies, waits for them, and re-layouts  4.62 us (5%)
    pallas_call x1, Pallas kernels, layer(): pl.pallas_call(layer_kernel, out_shape=(jax.ShapeDtypeStruct((T, COLS), B...  94.2 us
    unnamed x3, local copies, waits for them, and re-layouts  4.62 us

profile of v1, /device:TPU:1, one launch (start us, length us, event | category | flops | bytes accessed | tf_op | source)
XLA Modules:
  0.0 99.5 jit_solution(9004630221003156298)
XLA Ops:
  0.6 94.2 %layer.1 = (bf16[128,576]{1,0:T(8,128)(2,1)}, f32[36,256]{1,0:T(8,128)}, f32[36,512]{1,0:T(8,128)}) custom-call(bf16[128,2304]{1,0:T(8,128)(2,1)} %x_hbm.1, bf16[128,512]{1,0:T(8,128)(2,1)} %q_hbm.1, bf16[128,256]{1,0:T(8,128)(2,1)} %k_hbm.1, bf16[128,256]{1,0:T(8,128)(2,1)} %v_hbm.1, bf16[2304,512]{1,0:T(8,128)(2,1)} %wq_hbm.1, bf16[2304,256]{1,0:T(8,128)(2,1)} %wk_hbm.1, ...), custom_call_target="tpu_custom_call" | custom-call | tf_op jit(solution)/shard_map/layer/pallas_call | solution.py:533
  94.8 1.7 %copy.12 = bf16[128,576]{0,1:T(8,128)(2,1)} copy(bf16[128,576]{1,0:T(8,128)(2,1)} %get-tuple-element.9) | data formatting | bytes 294912
  96.5 1.4 %copy.15 = f32[36,256]{1,0:T(8,128)} copy(f32[36,256]{1,0:T(8,128)} %get-tuple-element.16) | data formatting | bytes 73728
  97.9 1.5 %copy.16 = f32[512,36]{0,1:T(8,128)} copy(f32[512,36]{0,1:T(8,128)} %bitcast.1) | data formatting | bytes 147456

commit v2 on v1

--- a/solution.py
+++ b/solution.py
@@ -20,7 +20,6 @@
 ROWS = 1024
 WIN = 640
 COLS = 576
-SPLIT = 5
 KEYS = 256
 NT = (((1,), (1,)), ((), ()))
 
@@ -42,11 +41,11 @@
     x_hbm, q_hbm, k_hbm, v_hbm, wq_hbm, wk_hbm, wv_hbm, wo_hbm, cot_hbm,
     gi_o, gwv_o, gwo_o,
     attn_o, gq_o, gk_o, gv_o, wq, wk, wv, win, winT, ag, gvg, po, pv, yo, yv, zso, zsv, zpo, zpv, zio, ziv, tb, hin,
-    kv, qg, dog, og, cot, wo, q2, do2, qT, doT, sbuf, dpbuf, pb_s, ds_s, ms, st, st_in, fin,
+    facc, kv, qg, dog, og, cot, wo, q2, do2, qT, doT, sbuf, dpbuf, pb_s, ds_s, ms, st, st_in, fin,
     oT, dqT, osend, oin, dqsend, dqin, dkv, rbuf, csend, cin, finkv, pin,
     lsem, pair_s, pair_r, q_s, q_r, do_s, do_r, kvx_s, kvy_s, kv_r, st_s, st_r, o_s, o_r, dq_s, dq_r,
     rb_s, rb_r, c_s, c_r, f_s, f_r,
-    w_s, w_r, ag_s, ag_r, gg_s, gg_r, yo_s, yo_r, yv_s, yv_r, zo_s, zo_r, zv_s, zv_r, h_s, h_r,
+    fx_s, fx_r, w_s, w_r, ag_s, ag_r, gg_s, gg_r, yo_s, yo_r, yv_s, yv_r, zo_s, zo_r, zv_s, zv_r, h_s, h_r,
 ):
     i, h, x, y, z = place()
     e, f = lax.rem(z, 2), lax.div(z, 2)
@@ -90,9 +89,22 @@
     hz = lax.rem(h + 2, 4)
     for to in ((i, hc), (i, hz)):
         pl.semaphore_signal(bar, inc=1, device_id=to, device_id_type=MESH)
-    pl.semaphore_wait(bar, 11)
-
     zp = z + 1 - 2 * e
+    for r in (1, 2, 3):
+        pl.semaphore_signal(bar, inc=1, device_id=dev(wrap(x + r), y, zp), device_id_type=MESH)
+    pl.semaphore_wait(bar, 14)
+
+    first = [
+        remote(src.at[:, pl.ds(col, D)], kv.at[4, n, pl.ds(erow, T), :], fx_s.at[m + n], fx_r.at[m + n], dev(wrap(x + 1), y, zt))
+        for m, col, zt in ((0, erow, z), (2, prow, zp))
+        for n, src in ((0, k_hbm), (1, v_hbm))
+    ]
+
+    @pl.when(x < 3)
+    def _():
+        for c in first:
+            c.start()
+
     pair = [
         remote(src.at[:, pl.ds(prow, D)], kv.at[0, n, pl.ds(erow, T), :], pair_s.at[n], pair_r.at[n], dev(x, y, zp))
         for n, src in ((0, k_hbm), (1, v_hbm))
@@ -140,10 +152,6 @@
             src, dst = jnp.where(up, 0, 8), jnp.where(up, yt - y, 8 + yt - y)
         return remote(kv.at[src], kv.at[dst], kvy_s.at[kind * 3 + r - 1], kv_r.at[dst], dev(x, yt, z))
 
-    @pl.when(x < 3)
-    def _():
-        fwd_x(0, 4).start()
-
     for r in (1, 2, 3):
         @pl.when(y + r < 4)
         def _():
@@ -154,7 +162,8 @@
 
     @pl.when(x >= 1)
     def _():
-        recv_slot(4)
+        for c in first:
+            c.wait_recv()
         for r in (1, 2, 3):
             fwd_y(r, 0).start()
 
@@ -175,6 +184,14 @@
     c_q.wait()
     for r in (1, 2, 3):
         qcopies[r - 1].wait_recv()
+    @pl.when(x >= 2)
+    def _():
+        recv_slot(8)
+        for r in (1, 2, 3):
+            @pl.when(y + r >= 4)
+            def _():
+                fwd_y(r, 1).start()
+
     for r in (1, 2, 3):
         docopies[r - 1].wait_recv()
 
@@ -189,14 +206,6 @@
             do2[rows, :] = db
             doT[:, rows] = db.T
 
-    @pl.when(x >= 2)
-    def _():
-        recv_slot(8)
-        for r in (1, 2, 3):
-            @pl.when(y + r >= 4)
-            def _():
-                fwd_y(r, 1).start()
-
     st[...] = jnp.concatenate([jnp.full((1, ROWS), NEG, F32), jnp.zeros((7, ROWS), F32)], axis=0)
     oT[...] = jnp.zeros_like(oT)
     dqT[...] = jnp.zeros_like(dqT)
@@ -206,15 +215,16 @@
             return 4 + jnp.where(r <= y, r, r - 4)
         return jnp.where(r <= y, r, r + 4)
 
-    @pl.loop(0, SLOTS)
+    @pl.loop(0, 12)
     def _(t):
-        d = jnp.where(
-            t < 2, t * 4, jnp.where(t == 8, 8, jnp.where(t < 5, slot_of(1, t - 1), slot_of(0, t - 4)))
-        )
-
-        @pl.when(S >= d)
-        def _():
-            @pl.when((t >= 2) & (t < 8))
+        kind = (t >= 5) & (t < 8)
+        r = jnp.where(t < 4, t, jnp.where(t < 8, t - 4, t - 8))
+        d = jnp.where(r == 0, t, jnp.where(kind, slot_of(0, r), slot_of(1, r)))
+        fits = (r == 0) | kind | jnp.where(t < 4, r <= y, r > y)
+
+        @pl.when((S >= d) & fits)
+        def _():
+            @pl.when(r > 0)
             def _():
                 recv_slot(d)
 
@@ -291,21 +301,23 @@
         n = kind * 3 + r - 1
         return remote(dkv.at[d], rbuf.at[n], rb_s.at[n], rb_r.at[n], dev(x, wrap(y - r), z))
 
-    def grad_step(t):
-        d = jnp.where(
-            t >= 6, 8 - (t - 6) * 4, jnp.where(t < 3, slot_of(0, t + 1), slot_of(1, t - 2))
-        )
-
-        @pl.when(S >= d)
+    @pl.loop(0, 12)
+    def _(t):
+        kind = (t >= 4) & (t < 7)
+        r = jnp.where(t < 3, t + 1, jnp.where(kind, t - 3, jnp.where((t >= 8) & (t < 11), t - 7, 0)))
+        d = jnp.where(r == 0, jnp.where(t == 3, 8, jnp.where(t == 7, 4, 0)), jnp.where(kind, slot_of(0, r), slot_of(1, r)))
+        fits = (r == 0) | kind | jnp.where(t < 3, r > y, r <= y)
+
+        @pl.when((S >= d) & fits)
         def _():
             grad_slot(d)
 
-            @pl.when(t < 6)
+            @pl.when(r > 0)
             def _():
-                r = lax.rem(t, 3) + 1
-                remote(dkv.at[d], rbuf.at[t], rb_s.at[t], rb_r.at[t], dev(x, wrap(y - r), z)).start()
-
-    pl.loop(0, SPLIT)(grad_step)
+                n = jnp.where(kind, r - 1, r + 2)
+                remote(dkv.at[d], rbuf.at[n], rb_s.at[n], rb_r.at[n], dev(x, wrap(y - r), z)).start()
+
+    dqcopies = spread(dqT, LOGIT_SCALE, dqsend, dqin, dq_s, dq_r)
 
     def over_x(src, dst, s, r_):
         return [remote(src, dst, s.at[r - 1], r_.at[r - 1], dev(wrap(x + r), y, z)) for r in (1, 2, 3)]
@@ -319,15 +331,14 @@
         c.start()
     ag[:, x] = attn_o[...]
 
-    pl.loop(SPLIT, SLOTS)(grad_step)
-
-    dqcopies = spread(dqT, LOGIT_SCALE, dqsend, dqin, dq_s, dq_r)
 
     def recv_back(n):
         remote(rbuf.at[n], rbuf.at[n], rb_s.at[n], rb_r.at[n], dev(x, wrap(y + 1), z)).wait_recv()
 
-    chain8 = remote(csend.at[0], cin.at[0], c_s.at[0], c_r.at[0], dev(wrap(x - 1), y, z))
-    chain4 = remote(csend.at[1], cin.at[1], c_s.at[1], c_r.at[1], dev(wrap(x - 1), y, z))
+    chain8, chain4 = (
+        [remote(csend.at[m, n], cin.at[m, n], c_s.at[m, n], c_r.at[m, n], dev(wrap(x - 1), y, z)) for n in range(2)]
+        for m in range(2)
+    )
 
     for c in c_win:
         c.wait()
@@ -341,36 +352,35 @@
                 cols = slice(b * 128, (b + 1) * 128)
                 winT[n, cols, pl.ds(pl.multiple_of(xx * T, T), T)] = win[n, xx, :, cols].T
 
-    for r in (1, 2, 3):
-        @pl.when((y + r < 4) | (x >= 2))
-        def _():
-            recv_back(3 + r - 1)
-
     @pl.when(x >= 2)
     def _():
+        facc[...] = dkv[8].astype(F32)
+        for r in (1, 2, 3):
+            @pl.when(y + r >= 4)
+            def _():
+                recv_back(3 + r - 1)
+                facc[...] += rbuf[3 + r - 1].astype(F32)
+
         for n in range(2):
-            acc = dkv[8, n].astype(F32)
-            for r in (1, 2, 3):
-                acc = acc + jnp.where(y + r >= 4, rbuf[3 + r - 1, n].astype(F32), 0.0)
-            csend[0, n] = acc.astype(BF16)
-        chain8.start()
+            csend[0, n] = facc[n].astype(BF16)
+            chain8[n].start()
 
     @pl.when(x >= 1)
     def _():
         for r in (1, 2, 3):
             recv_back(r - 1)
 
-        @pl.when(x < 3)
-        def _():
-            chain8.wait_recv()
-
         for n in range(2):
+            @pl.when(x < 3)
+            def _():
+                chain8[n].wait_recv()
+
             acc = dkv[4, n].astype(F32)
             for r in (1, 2, 3):
                 acc = acc + rbuf[r - 1, n].astype(F32)
             acc = acc + jnp.where(x < 3, cin[0, n].astype(F32), 0.0)
             csend[1, n] = acc.astype(BF16)
-        chain4.start()
+            chain4[n].start()
 
     off = pl.multiple_of(64 * lax.rem(x, 2), 16)
 
@@ -390,21 +400,30 @@
     for c in yocopies:
         c.start()
 
-    @pl.when(x < 3)
-    def _():
-        chain4.wait_recv()
-
-    for n in range(2):
-        acc = dkv[0, n].astype(F32)
-        for r in (1, 2, 3):
-            acc = acc + jnp.where(y + r < 4, rbuf[3 + r - 1, n].astype(F32), 0.0)
-        acc = acc + jnp.where(x < 3, cin[1, n].astype(F32), 0.0)
-        finkv[n] = acc.astype(BF16)
+    facc[...] = dkv[0].astype(F32)
+    for r in (1, 2, 3):
+        @pl.when(y + r < 4)
+        def _():
+            recv_back(3 + r - 1)
+            facc[...] += rbuf[3 + r - 1].astype(F32)
 
     swap = [
         remote(finkv.at[n, pl.ds(prow, T), :], pin.at[n], f_s.at[n], f_r.at[n], dev(x, y, zp)) for n in range(2)
     ]
-    for c in swap:
+    ggcopies = [
+        remote(finkv.at[1, pl.ds(row, T), :], gvg.at[e, x], gg_s.at[m + r - 1], gg_r.at[m + r - 1], dev(wrap(x + r), y, zt))
+        for r in (1, 2, 3)
+        for m, row, zt in ((0, erow, z), (3, prow, zp))
+    ]
+    for n in range(2):
+        @pl.when(x < 3)
+        def _():
+            chain4[n].wait_recv()
+
+        acc = facc[n] + jnp.where(x < 3, cin[1, n].astype(F32), 0.0)
+        finkv[n] = acc.astype(BF16)
+        swap[n].start()
+    for c in ggcopies:
         c.start()
 
     for c in dqcopies:
@@ -418,18 +437,15 @@
     for n, out in ((0, gk_o), (1, gv_o)):
         out[e] = finkv[n, pl.ds(erow, T), :]
         out[1 - e] = pin[n]
-    ggcopies = over_x(gv_o, gvg.at[:, x], gg_s, gg_r)
-    for c in ggcopies:
-        c.start()
     gvg[:, x] = gv_o[...]
 
     def terms(hh):
         rows = pl.ds(pl.multiple_of(COLS * hh, 16), COLS)
-        acc = jnp.zeros((T, COLS), F32)
+        acc = jnp.zeros((COLS, T), F32)
         for n in range(2):
-            acc = acc + lax.dot_general(gq_o[n], wq[rows, n * 256 : (n + 1) * 256], NT, preferred_element_type=F32)
-            acc = acc + lax.dot_general(gk_o[n], wk[rows, n * D : (n + 1) * D], NT, preferred_element_type=F32)
-            acc = acc + lax.dot_general(gv_o[n], wv[rows, n * D : (n + 1) * D], NT, preferred_element_type=F32)
+            acc = acc + lax.dot_general(wq[rows, n * 256 : (n + 1) * 256], gq_o[n], NT, preferred_element_type=F32)
+            acc = acc + lax.dot_general(wk[rows, n * D : (n + 1) * D], gk_o[n], NT, preferred_element_type=F32)
+            acc = acc + lax.dot_general(wv[rows, n * D : (n + 1) * D], gv_o[n], NT, preferred_element_type=F32)
         return acc
 
     hzc = lax.rem(hc + 2, 4)
@@ -437,22 +453,6 @@
     far = remote(tb.at[0], hin.at[0], h_s.at[0], h_r.at[0], (i, hc))
     far.start()
     mine_far = terms(hz)
-    far.wait_recv()
-    tb[1] = (mine_far + hin[0].astype(F32)).astype(BF16)
-    across = remote(tb.at[1], hin.at[1], h_s.at[1], h_r.at[1], (i, hz))
-    across.start()
-    tb[2] = terms(hc).astype(BF16)
-    near = remote(tb.at[2], hin.at[2], h_s.at[2], h_r.at[2], (i, hc))
-    near.start()
-
-    for c in ggcopies:
-        c.wait_recv()
-    for n in range(2):
-        pv[:, n * D : (n + 1) * D] = dot(winT[0], gvg[n].reshape(4 * T, D)).astype(BF16)
-    yvcopies = over_y(pv, yv, yv_s, yv_r)
-    for c in yvcopies:
-        c.start()
-
     def over_z(copies, own, buf, total_s, piece_s, in_s, s, r_):
         for c in copies:
             c.wait_recv()
@@ -461,7 +461,7 @@
             acc = acc + buf[r].astype(F32)
         total_s[...] = acc
         for zz in range(4):
-            piece_s[zz] = total_s[36 * zz : 36 * (zz + 1), :]
+            piece_s[zz] = total_s[36 * zz : 36 * (zz + 1), :].astype(piece_s.dtype)
         out = []
         for r in (1, 2, 3):
             zt = wrap(z + r)
@@ -471,14 +471,30 @@
         return out
 
     zocopies = over_z(yocopies, po, yo, zso, zpo, zio, zo_s, zo_r)
+    far.wait_recv()
+    tb[1] = (mine_far + hin[0].astype(F32)).astype(BF16)
+    across = remote(tb.at[1], hin.at[1], h_s.at[1], h_r.at[1], (i, hz))
+    across.start()
+    tb[2] = terms(hc).astype(BF16)
+    near = remote(tb.at[2], hin.at[2], h_s.at[2], h_r.at[2], (i, hc))
+    near.start()
+
+    for c in ggcopies:
+        c.wait_recv()
+    for n in range(2):
+        pv[:, n * D : (n + 1) * D] = dot(winT[0], gvg[n].reshape(4 * T, D)).astype(BF16)
+    yvcopies = over_y(pv, yv, yv_s, yv_r)
+    for c in yvcopies:
+        c.start()
+
     mine_near = terms(h)
     zvcopies = over_z(yvcopies, pv, yv, zsv, zpv, ziv, zv_s, zv_r)
 
     for c in zocopies:
         c.wait_recv()
-    acc = zpo[z]
+    acc = zpo[z].astype(F32)
     for r in range(3):
-        acc = acc + zio[r]
+        acc = acc + zio[r].astype(F32)
     gwo_o[...] = acc
     near.wait_recv()
     across.wait_recv()
@@ -498,7 +514,8 @@
 
     @pl.when(x < 3)
     def _():
-        fwd_x(0, 4).wait_send()
+        for c in first:
+            c.wait_send()
 
     @pl.when((x >= 1) & (x < 3))
     def _():
@@ -520,11 +537,13 @@
 
     @pl.when(x >= 2)
     def _():
-        chain8.wait_send()
+        for c in chain8:
+            c.wait_send()
 
     @pl.when(x >= 1)
     def _():
-        chain4.wait_send()
+        for c in chain4:
+            c.wait_send()
 
 
 def layer(xn, q, k, v, wq, wk, wv, wo, cot):
@@ -533,7 +552,7 @@
     return pl.pallas_call(
         layer_kernel,
         out_shape=(
-            jax.ShapeDtypeStruct((T, COLS), BF16),
+            jax.ShapeDtypeStruct((COLS, T), BF16),
             jax.ShapeDtypeStruct((36, 256), F32),
             jax.ShapeDtypeStruct((36, 512), F32),
         ),
@@ -557,12 +576,13 @@
             vm((3, 144, 256), BF16),
             vm((144, 512), F32),
             vm((144, 256), F32),
-            vm((4, 36, 512), F32),
+            vm((4, 36, 512), BF16),
             vm((4, 36, 256), F32),
-            vm((3, 36, 512), F32),
+            vm((3, 36, 512), BF16),
             vm((3, 36, 256), F32),
-            vm((3, T, COLS), BF16),
-            vm((3, T, COLS), BF16),
+            vm((3, COLS, T), BF16),
+            vm((3, COLS, T), BF16),
+            vm((2, KEYS, D), F32),
             vm((SLOTS, 2, KEYS, D), BF16),
             vm((4, T, 256), BF16),
             vm((4, T, 256), BF16),
@@ -595,8 +615,8 @@
             vm((2, T, D), BF16),
             dma((10,)), dma((2,)), dma((2,)), dma((3,)), dma((3,)), dma((3,)), dma((3,)),
             dma((2,)), dma((6,)), dma((SLOTS,)), dma, dma, dma((3,)), dma((3,)), dma((3,)), dma((3,)),
-            dma((6,)), dma((6,)), dma((2,)), dma((2,)), dma((2,)), dma((2,)),
-            dma((2, 3)), dma((2, 3)), *([dma((3,))] * 14),
+            dma((6,)), dma((6,)), dma((2, 2)), dma((2, 2)), dma((2,)), dma((2,)),
+            dma((4,)), dma((4,)), dma((2, 3)), dma((2, 3)), *([dma((3,))] * 2), *([dma((6,))] * 2), *([dma((3,))] * 10),
         ],
         compiler_params=pltpu.CompilerParams(
             collective_id=1, has_side_effects=True, vmem_limit_bytes=62 * 1024 * 1024
@@ -605,9 +625,22 @@
     )(xn, q, k, v, wq, wk, wv, wo, cot)
 
 
+def hand_over(*refs):
+    for n in range(3):
+        refs[3 + n][...] = refs[n][...]
+
+
 def local(*args):
-    grad_input, grad_wvalue, grad_woutput = layer(*args)
-    return grad_input, grad_wvalue, grad_woutput.T
+    results = layer(*args)
+    vmem = tuple(pl.BlockSpec(memory_space=pltpu.VMEM) for _ in range(3))
+    grad_input, grad_wvalue, grad_woutput = pl.pallas_call(
+        hand_over,
+        out_shape=tuple(jax.ShapeDtypeStruct(a.shape, a.dtype) for a in results),
+        in_specs=vmem,
+        out_specs=vmem,
+        name="hand_over",
+    )(*results)
+    return grad_input.T, grad_wvalue, grad_woutput.T
 
 
 def solution(mesh):

time: 99.7 us -> 79.3 us (0.80)
  Pallas kernels: 94.2 us -> 78.6 us
  local copies, waits for them, and re-layouts: 4.62 us -> 0 us
    pallas_call x1 -> x2, Pallas kernels: 94.2 us -> 78.6 us  [the longest x1 76.9 us: layer(): pl.pallas_call(layer_kernel, out_shape=(jax.ShapeDtypeStruct((COLS, T), B...]
    unnamed x3 -> x0, local copies, waits for them, and re-layouts: 4.62 us -> none
where the time goes in v2:
time: 79.3 us; the launch traced here: 79.2 us
  Pallas kernels  78.6 us (99%)
    pallas_call x1, Pallas kernels, layer(): pl.pallas_call(layer_kernel, out_shape=(jax.ShapeDtypeStruct((COLS, T), B...  76.9 us
    pallas_call x1, Pallas kernels, local(): pl.pallas_call(hand_over, out_shape=tuple((jax.ShapeDtypeStruct(a.shape,...  1.68 us

profile of v2, /device:TPU:1, one launch (start us, length us, event | category | flops | bytes accessed | tf_op | source)
XLA Modules:
  0.0 79.2 jit_solution(12287638972830063971)
XLA Ops:
  0.6 76.9 %layer.1 = (bf16[576,128]{1,0:T(8,128)(2,1)}, f32[36,256]{1,0:T(8,128)}, f32[36,512]{1,0:T(8,128)}) custom-call(bf16[128,2304]{1,0:T(8,128)(2,1)} %x_hbm.1, bf16[128,512]{1,0:T(8,128)(2,1)} %q_hbm.1, bf16[128,256]{1,0:T(8,128)(2,1)} %k_hbm.1, bf16[128,256]{1,0:T(8,128)(2,1)} %v_hbm.1, bf16[2304,512]{1,0:T(8,128)(2,1)} %wq_hbm.1, bf16[2304,256]{1,0:T(8,128)(2,1)} %wk_hbm.1, ...), custom_call_target="tpu_custom_call" | custom-call | tf_op jit(solution)/shard_map/layer/pallas_call | solution.py:552
  77.5 1.7 %hand_over.1 = (bf16[576,128]{1,0:T(8,128)(2,1)}, f32[36,256]{1,0:T(8,128)}, f32[36,512]{1,0:T(8,128)}) custom-call(bf16[576,128]{1,0:T(8,128)(2,1)} %get-tuple-element.9.refs_0_, f32[36,256]{1,0:T(8,128)} %get-tuple-element.10.refs_1_, f32[36,512]{1,0:T(8,128)} %get-tuple-element.11.refs_2_), custom_call_target="tpu_custom_call" | custom-call | tf_op jit(solution)/shard_map/hand_over/pallas_call | solution.py:636

commit v3 on v2

--- a/solution.py
+++ b/solution.py
@@ -41,7 +41,7 @@
     x_hbm, q_hbm, k_hbm, v_hbm, wq_hbm, wk_hbm, wv_hbm, wo_hbm, cot_hbm,
     gi_o, gwv_o, gwo_o,
     attn_o, gq_o, gk_o, gv_o, wq, wk, wv, win, winT, ag, gvg, po, pv, yo, yv, zso, zsv, zpo, zpv, zio, ziv, tb, hin,
-    facc, kv, qg, dog, og, cot, wo, q2, do2, qT, doT, sbuf, dpbuf, pb_s, ds_s, ms, st, st_in, fin,
+    tq, facc, kv, qg, dog, og, cot, wo, q2, do2, qT, doT, sbuf, dpbuf, pb_s, ds_s, ms, st, st_in, fin,
     oT, dqT, osend, oin, dqsend, dqin, dkv, rbuf, csend, cin, finkv, pin,
     lsem, pair_s, pair_r, q_s, q_r, do_s, do_r, kvx_s, kvy_s, kv_r, st_s, st_r, o_s, o_r, dq_s, dq_r,
     rb_s, rb_r, c_s, c_r, f_s, f_r,
@@ -94,6 +94,13 @@
         pl.semaphore_signal(bar, inc=1, device_id=dev(wrap(x + r), y, zp), device_id_type=MESH)
     pl.semaphore_wait(bar, 14)
 
+    pair = [
+        remote(src.at[:, pl.ds(prow, D)], kv.at[0, n, pl.ds(erow, T), :], pair_s.at[n], pair_r.at[n], dev(x, y, zp))
+        for n, src in ((0, k_hbm), (1, v_hbm))
+    ]
+    for c in pair:
+        c.start()
+
     first = [
         remote(src.at[:, pl.ds(col, D)], kv.at[4, n, pl.ds(erow, T), :], fx_s.at[m + n], fx_r.at[m + n], dev(wrap(x + 1), y, zt))
         for m, col, zt in ((0, erow, z), (2, prow, zp))
@@ -104,13 +111,6 @@
     def _():
         for c in first:
             c.start()
-
-    pair = [
-        remote(src.at[:, pl.ds(prow, D)], kv.at[0, n, pl.ds(erow, T), :], pair_s.at[n], pair_r.at[n], dev(x, y, zp))
-        for n, src in ((0, k_hbm), (1, v_hbm))
-    ]
-    for c in pair:
-        c.start()
 
     def gathered(src_of, buf, s, r_):
         copies = []
@@ -301,8 +301,7 @@
         n = kind * 3 + r - 1
         return remote(dkv.at[d], rbuf.at[n], rb_s.at[n], rb_r.at[n], dev(x, wrap(y - r), z))
 
-    @pl.loop(0, 12)
-    def _(t):
+    def grad_step(t):
         kind = (t >= 4) & (t < 7)
         r = jnp.where(t < 3, t + 1, jnp.where(kind, t - 3, jnp.where((t >= 8) & (t < 11), t - 7, 0)))
         d = jnp.where(r == 0, jnp.where(t == 3, 8, jnp.where(t == 7, 4, 0)), jnp.where(kind, slot_of(0, r), slot_of(1, r)))
@@ -317,6 +316,36 @@
                 n = jnp.where(kind, r - 1, r + 2)
                 remote(dkv.at[d], rbuf.at[n], rb_s.at[n], rb_r.at[n], dev(x, wrap(y - r), z)).start()
 
+    pl.loop(0, 8)(grad_step)
+
+    def recv_back(n):
+        remote(rbuf.at[n], rbuf.at[n], rb_s.at[n], rb_r.at[n], dev(x, wrap(y + 1), z)).wait_recv()
+
+    chain8, chain4 = (
+        [
+            remote(
+                csend.at[m, :, pl.ds(row, T), :], cin.at[m, part], c_s.at[m, part], c_r.at[m, part], dev(wrap(x - 2 + m), y, zt)
+            )
+            for part, row, zt in ((0, erow, z), (1, prow, zp))
+        ]
+        for m in range(2)
+    )
+
+    @pl.when(x >= 2)
+    def _():
+        facc[...] = dkv[8].astype(F32)
+        for r in (1, 2, 3):
+            @pl.when(y + r >= 4)
+            def _():
+                recv_back(3 + r - 1)
+                facc[...] += rbuf[3 + r - 1].astype(F32)
+
+        csend[0] = facc[...].astype(BF16)
+        for c in chain8:
+            c.start()
+
+    pl.loop(8, 12)(grad_step)
+
     dqcopies = spread(dqT, LOGIT_SCALE, dqsend, dqin, dq_s, dq_r)
 
     def over_x(src, dst, s, r_):
@@ -331,14 +360,6 @@
         c.start()
     ag[:, x] = attn_o[...]
 
-
-    def recv_back(n):
-        remote(rbuf.at[n], rbuf.at[n], rb_s.at[n], rb_r.at[n], dev(x, wrap(y + 1), z)).wait_recv()
-
-    chain8, chain4 = (
-        [remote(csend.at[m, n], cin.at[m, n], c_s.at[m, n], c_r.at[m, n], dev(wrap(x - 1), y, z)) for n in range(2)]
-        for m in range(2)
-    )
 
     for c in c_win:
         c.wait()
@@ -352,35 +373,15 @@
                 cols = slice(b * 128, (b + 1) * 128)
                 winT[n, cols, pl.ds(pl.multiple_of(xx * T, T), T)] = win[n, xx, :, cols].T
 
-    @pl.when(x >= 2)
-    def _():
-        facc[...] = dkv[8].astype(F32)
-        for r in (1, 2, 3):
-            @pl.when(y + r >= 4)
-            def _():
-                recv_back(3 + r - 1)
-                facc[...] += rbuf[3 + r - 1].astype(F32)
-
-        for n in range(2):
-            csend[0, n] = facc[n].astype(BF16)
-            chain8[n].start()
-
     @pl.when(x >= 1)
     def _():
+        facc[...] = dkv[4].astype(F32)
         for r in (1, 2, 3):
             recv_back(r - 1)
-
-        for n in range(2):
-            @pl.when(x < 3)
-            def _():
-                chain8[n].wait_recv()
-
-            acc = dkv[4, n].astype(F32)
-            for r in (1, 2, 3):
-                acc = acc + rbuf[r - 1, n].astype(F32)
-            acc = acc + jnp.where(x < 3, cin[0, n].astype(F32), 0.0)
-            csend[1, n] = acc.astype(BF16)
-            chain4[n].start()
+            facc[...] += rbuf[r - 1].astype(F32)
+        csend[1] = facc[...].astype(BF16)
+        for c in chain4:
+            c.start()
 
     off = pl.multiple_of(64 * lax.rem(x, 2), 16)
 
@@ -392,6 +393,34 @@
             copies.append(remote(src.at[rows, :], buf.at[r - 1], s.at[r - 1], r_.at[r - 1], dev(x, yt, z)))
         return copies
 
+    facc[...] = dkv[0].astype(F32)
+    for r in (1, 2, 3):
+        @pl.when(y + r < 4)
+        def _():
+            recv_back(3 + r - 1)
+            facc[...] += rbuf[3 + r - 1].astype(F32)
+
+    finkv[...] = facc[:, pl.ds(prow, T), :].astype(BF16)
+    swap = [remote(finkv, pin, f_s, f_r, dev(x, y, zp))]
+    swap[0].start()
+
+    for c in dqcopies:
+        c.wait_recv()
+    for n in range(2):
+        gq_o[n] = (dqin[n].astype(F32) + dqin[n + 2].astype(F32)).astype(BF16)
+    for c in c_w:
+        c.wait()
+
+    def wrows(hh):
+        return pl.ds(pl.multiple_of(COLS * hh, 16), COLS)
+
+    @pl.loop(0, 4)
+    def _(hh):
+        tq[hh] = sum(
+            lax.dot_general(wq[wrows(hh), n * 256 : (n + 1) * 256], gq_o[n], NT, preferred_element_type=F32)
+            for n in range(2)
+        )
+
     for c in agcopies:
         c.wait_recv()
     for n in range(2):
@@ -400,59 +429,55 @@
     for c in yocopies:
         c.start()
 
-    facc[...] = dkv[0].astype(F32)
-    for r in (1, 2, 3):
-        @pl.when(y + r < 4)
-        def _():
-            recv_back(3 + r - 1)
-            facc[...] += rbuf[3 + r - 1].astype(F32)
-
-    swap = [
-        remote(finkv.at[n, pl.ds(prow, T), :], pin.at[n], f_s.at[n], f_r.at[n], dev(x, y, zp)) for n in range(2)
-    ]
-    ggcopies = [
-        remote(finkv.at[1, pl.ds(row, T), :], gvg.at[e, x], gg_s.at[m + r - 1], gg_r.at[m + r - 1], dev(wrap(x + r), y, zt))
-        for r in (1, 2, 3)
-        for m, row, zt in ((0, erow, z), (3, prow, zp))
-    ]
-    for n in range(2):
-        @pl.when(x < 3)
-        def _():
-            chain4[n].wait_recv()
-
-        acc = facc[n] + jnp.where(x < 3, cin[1, n].astype(F32), 0.0)
-        finkv[n] = acc.astype(BF16)
-        swap[n].start()
+    swap[0].wait_recv()
+    final = [[facc[n, pl.ds(erow, T), :], pin[n].astype(F32)] for n in range(2)]
+    for m in (0, 1):
+        chain = (chain8, chain4)[m]
+
+        @pl.when(x < 2 + m)
+        def _():
+            for c in chain:
+                c.wait_recv()
+
+        for n in range(2):
+            for part in range(2):
+                final[n][part] = final[n][part] + jnp.where(x < 2 + m, cin[m, part, n].astype(F32), 0.0)
+    for n, out in ((1, gv_o), (0, gk_o)):
+        out[e] = final[n][0].astype(BF16)
+        out[1 - e] = final[n][1].astype(BF16)
+    ggcopies = over_x(gv_o, gvg.at[:, x], gg_s, gg_r)
     for c in ggcopies:
         c.start()
-
-    for c in dqcopies:
-        c.wait_recv()
-    for n in range(2):
-        gq_o[n] = (dqin[n].astype(F32) + dqin[n + 2].astype(F32)).astype(BF16)
-    for c in c_w:
-        c.wait()
-    for c in swap:
-        c.wait_recv()
-    for n, out in ((0, gk_o), (1, gv_o)):
-        out[e] = finkv[n, pl.ds(erow, T), :]
-        out[1 - e] = pin[n]
     gvg[:, x] = gv_o[...]
 
     def terms(hh):
-        rows = pl.ds(pl.multiple_of(COLS * hh, 16), COLS)
-        acc = jnp.zeros((COLS, T), F32)
+        acc = tq[hh]
         for n in range(2):
-            acc = acc + lax.dot_general(wq[rows, n * 256 : (n + 1) * 256], gq_o[n], NT, preferred_element_type=F32)
-            acc = acc + lax.dot_general(wk[rows, n * D : (n + 1) * D], gk_o[n], NT, preferred_element_type=F32)
-            acc = acc + lax.dot_general(wv[rows, n * D : (n + 1) * D], gv_o[n], NT, preferred_element_type=F32)
+            acc = acc + lax.dot_general(wk[wrows(hh), n * D : (n + 1) * D], gk_o[n], NT, preferred_element_type=F32)
+            acc = acc + lax.dot_general(wv[wrows(hh), n * D : (n + 1) * D], gv_o[n], NT, preferred_element_type=F32)
         return acc
 
     hzc = lax.rem(hc + 2, 4)
     tb[0] = terms(hzc).astype(BF16)
     far = remote(tb.at[0], hin.at[0], h_s.at[0], h_r.at[0], (i, hc))
     far.start()
+    for c in ggcopies:
+        c.wait_recv()
+    for n in range(2):
+        pv[:, n * D : (n + 1) * D] = dot(winT[0], gvg[n].reshape(4 * T, D)).astype(BF16)
+    yvcopies = over_y(pv, yv, yv_s, yv_r)
+    for c in yvcopies:
+        c.start()
+
     mine_far = terms(hz)
+    far.wait_recv()
+    tb[1] = (mine_far + hin[0].astype(F32)).astype(BF16)
+    across = remote(tb.at[1], hin.at[1], h_s.at[1], h_r.at[1], (i, hz))
+    across.start()
+    tb[2] = terms(hc).astype(BF16)
+    near = remote(tb.at[2], hin.at[2], h_s.at[2], h_r.at[2], (i, hc))
+    near.start()
+
     def over_z(copies, own, buf, total_s, piece_s, in_s, s, r_):
         for c in copies:
             c.wait_recv()
@@ -471,22 +496,6 @@
         return out
 
     zocopies = over_z(yocopies, po, yo, zso, zpo, zio, zo_s, zo_r)
-    far.wait_recv()
-    tb[1] = (mine_far + hin[0].astype(F32)).astype(BF16)
-    across = remote(tb.at[1], hin.at[1], h_s.at[1], h_r.at[1], (i, hz))
-    across.start()
-    tb[2] = terms(hc).astype(BF16)
-    near = remote(tb.at[2], hin.at[2], h_s.at[2], h_r.at[2], (i, hc))
-    near.start()
-
-    for c in ggcopies:
-        c.wait_recv()
-    for n in range(2):
-        pv[:, n * D : (n + 1) * D] = dot(winT[0], gvg[n].reshape(4 * T, D)).astype(BF16)
-    yvcopies = over_y(pv, yv, yv_s, yv_r)
-    for c in yvcopies:
-        c.start()
-
     mine_near = terms(h)
     zvcopies = over_z(yvcopies, pv, yv, zsv, zpv, ziv, zv_s, zv_r)
 
@@ -501,9 +510,9 @@
     gi_o[...] = (mine_near + hin[2].astype(F32) + hin[1].astype(F32)).astype(BF16)
     for c in zvcopies:
         c.wait_recv()
-    acc = zpv[z]
+    acc = zpv[z].astype(F32)
     for r in range(3):
-        acc = acc + ziv[r]
+        acc = acc + ziv[r].astype(F32)
     gwv_o[...] = acc
 
     for c in (
@@ -577,11 +586,12 @@
             vm((144, 512), F32),
             vm((144, 256), F32),
             vm((4, 36, 512), BF16),
-            vm((4, 36, 256), F32),
+            vm((4, 36, 256), BF16),
             vm((3, 36, 512), BF16),
-            vm((3, 36, 256), F32),
+            vm((3, 36, 256), BF16),
             vm((3, COLS, T), BF16),
             vm((3, COLS, T), BF16),
+            vm((4, COLS, T), F32),
             vm((2, KEYS, D), F32),
             vm((SLOTS, 2, KEYS, D), BF16),
             vm((4, T, 256), BF16),
@@ -610,13 +620,13 @@
             vm((SLOTS, 2, KEYS, D), BF16),
             vm((6, 2, KEYS, D), BF16),
             vm((2, 2, KEYS, D), BF16),
-            vm((2, 2, KEYS, D), BF16),
-            vm((2, KEYS, D), BF16),
+            vm((2, 2, 2, T, D), BF16),
+            vm((2, T, D), BF16),
             vm((2, T, D), BF16),
             dma((10,)), dma((2,)), dma((2,)), dma((3,)), dma((3,)), dma((3,)), dma((3,)),
             dma((2,)), dma((6,)), dma((SLOTS,)), dma, dma, dma((3,)), dma((3,)), dma((3,)), dma((3,)),
-            dma((6,)), dma((6,)), dma((2, 2)), dma((2, 2)), dma((2,)), dma((2,)),
-            dma((4,)), dma((4,)), dma((2, 3)), dma((2, 3)), *([dma((3,))] * 2), *([dma((6,))] * 2), *([dma((3,))] * 10),
+            dma((6,)), dma((6,)), dma((2, 2)), dma((2, 2)), dma, dma,
+            dma((4,)), dma((4,)), dma((2, 3)), dma((2, 3)), *([dma((3,))] * 2), *([dma((3,))] * 2), *([dma((3,))] * 10),
         ],
         compiler_params=pltpu.CompilerParams(
             collective_id=1, has_side_effects=True, vmem_limit_bytes=62 * 1024 * 1024

time: 79.3 us -> 83 us (1.047)
  the two profiles are of different devices: /device:TPU:1 before, /device:TPU:4 now
where the time goes in v3:
time: 83 us; the launch traced here: 82.9 us
  Pallas kernels  82.2 us (99%)
    pallas_call x1, Pallas kernels, layer(): pl.pallas_call(layer_kernel, out_shape=(jax.ShapeDtypeStruct((COLS, T), B...  80.6 us
    pallas_call x1, Pallas kernels, local(): pl.pallas_call(hand_over, out_shape=tuple((jax.ShapeDtypeStruct(a.shape,...  1.68 us

profile of v3, /device:TPU:4, one launch (start us, length us, event | category | flops | bytes accessed | tf_op | source)
XLA Modules:
  0.0 82.9 jit_solution(15963020270411586683)
XLA Ops:
  0.6 80.6 %layer.1 = (bf16[576,128]{1,0:T(8,128)(2,1)}, f32[36,256]{1,0:T(8,128)}, f32[36,512]{1,0:T(8,128)}) custom-call(bf16[128,2304]{1,0:T(8,128)(2,1)} %x_hbm.1, bf16[128,512]{1,0:T(8,128)(2,1)} %q_hbm.1, bf16[128,256]{1,0:T(8,128)(2,1)} %k_hbm.1, bf16[128,256]{1,0:T(8,128)(2,1)} %v_hbm.1, bf16[2304,512]{1,0:T(8,128)(2,1)} %wq_hbm.1, bf16[2304,256]{1,0:T(8,128)(2,1)} %wk_hbm.1, ...), custom_call_target="tpu_custom_call" | custom-call | tf_op jit(solution)/shard_map/layer/pallas_call | solution.py:561
  81.2 1.7 %hand_over.1 = (bf16[576,128]{1,0:T(8,128)(2,1)}, f32[36,256]{1,0:T(8,128)}, f32[36,512]{1,0:T(8,128)}) custom-call(bf16[576,128]{1,0:T(8,128)(2,1)} %get-tuple-element.9.refs_0_, f32[36,256]{1,0:T(8,128)} %get-tuple-element.10.refs_1_, f32[36,512]{1,0:T(8,128)} %get-tuple-element.11.refs_2_), custom_call_target="tpu_custom_call" | custom-call | tf_op jit(solution)/shard_map/hand_over/pallas_call | solution.py:646

commit v4 on v3

--- a/solution.py
+++ b/solution.py
@@ -178,22 +178,10 @@
             wcopies.append(
                 remote(src.at[:, window(xt)], win.at[n, x], w_s.at[n, r - 1], w_r.at[n, r - 1], dev(xt, y, z))
             )
-    for c in wcopies + c_win + c_w:
-        c.start()
 
     c_q.wait()
-    for r in (1, 2, 3):
-        qcopies[r - 1].wait_recv()
-    @pl.when(x >= 2)
-    def _():
-        recv_slot(8)
-        for r in (1, 2, 3):
-            @pl.when(y + r >= 4)
-            def _():
-                fwd_y(r, 1).start()
-
-    for r in (1, 2, 3):
-        docopies[r - 1].wait_recv()
+    for c in qcopies:
+        c.wait_recv()
 
     @pl.loop(0, 4)
     def _(zz):
@@ -202,9 +190,6 @@
             qb = qg[zz, :, j * D : (j + 1) * D]
             q2[rows, :] = qb
             qT[:, rows] = qb.T
-            db = dog[zz, :, j * D : (j + 1) * D]
-            do2[rows, :] = db
-            doT[:, rows] = db.T
 
     st[...] = jnp.concatenate([jnp.full((1, ROWS), NEG, F32), jnp.zeros((7, ROWS), F32)], axis=0)
     oT[...] = jnp.zeros_like(oT)
@@ -215,45 +200,85 @@
             return 4 + jnp.where(r <= y, r, r - 4)
         return jnp.where(r <= y, r, r + 4)
 
-    @pl.loop(0, 12)
-    def _(t):
-        kind = (t >= 5) & (t < 8)
-        r = jnp.where(t < 4, t, jnp.where(t < 8, t - 4, t - 8))
-        d = jnp.where(r == 0, t, jnp.where(kind, slot_of(0, r), slot_of(1, r)))
-        fits = (r == 0) | kind | jnp.where(t < 4, r <= y, r > y)
-
-        @pl.when((S >= d) & fits)
-        def _():
-            @pl.when(r > 0)
-            def _():
-                recv_slot(d)
-
-            kd = kv[d, 0]
-            vd = kv[d, 1]
-            vt = vd.T
-            low = jnp.where(d == 0, 0, -100000)
-            high = jnp.where(d == 8, 0, 100000)
-            for c in range(4):
-                cs = slice(c * 256, (c + 1) * 256)
-                s = dot(kd, qT[:, cs])
+    def probabilities(d, edge):
+        kd = kv[d, 0]
+        vt = kv[d, 1].T
+        low = jnp.where(d == 0, 0, -100000)
+        high = jnp.where(d == 8, 0, 100000)
+        for c in range(4):
+            cs = slice(c * 256, (c + 1) * 256)
+            s = dot(kd, qT[:, cs])
+            if edge:
                 gap = (
                     lax.broadcasted_iota(jnp.int32, (KEYS, 256), 1)
                     - lax.broadcasted_iota(jnp.int32, (KEYS, 256), 0)
                     + ((c % 2) * 256 - f * 256)
                 )
                 s = jnp.where((gap >= low) & (gap < high), s, NEG)
-                before = st[0:1, cs]
-                top = jnp.maximum(before, jnp.max(s, axis=0, keepdims=True))
-                p = jnp.exp2((s - top) * EXP2_SCALE)
-                keep = jnp.exp2((before - top) * EXP2_SCALE)
+            before = st[0:1, cs]
+            top = jnp.maximum(before, jnp.max(s, axis=0, keepdims=True))
+            p = jnp.exp2((s - top) * EXP2_SCALE)
+            keep = jnp.exp2((before - top) * EXP2_SCALE)
+            st[0:1, cs] = top
+            st[1:2, cs] = st[1:2, cs] * keep + jnp.sum(p, axis=0, keepdims=True)
+            ms[d, 0:1, cs] = top
+            sbuf[d, :, cs] = p
+            oT[:, cs] = oT[:, cs] * keep + dot(vt, p.astype(BF16))
+
+    def prob_step(t):
+        kind = (t >= 5) & (t < 8)
+        r = jnp.where(t < 4, t, jnp.where(t < 8, t - 4, t - 8))
+        d = jnp.where(r == 0, t, jnp.where(kind, slot_of(0, r), slot_of(1, r)))
+        fits = (r == 0) | kind | jnp.where(t < 4, r <= y, r > y)
+
+        @pl.when((S >= d) & fits & (r == 0) & (t != 4))
+        def _():
+            probabilities(d, True)
+
+        @pl.when((S >= d) & fits & ((r > 0) | (t == 4)))
+        def _():
+            @pl.when(r > 0)
+            def _():
+                recv_slot(d)
+
+            probabilities(d, False)
+
+    pl.loop(0, 5)(prob_step)
+
+    @pl.when(x >= 2)
+    def _():
+        recv_slot(8)
+        for r in (1, 2, 3):
+            @pl.when(y + r >= 4)
+            def _():
+                fwd_y(r, 1).start()
+
+    pl.loop(5, 12)(prob_step)
+
+    for c in docopies:
+        c.wait_recv()
+    for c in wcopies + c_win + c_w:
+        c.start()
+
+    @pl.loop(0, 4)
+    def _(zz):
+        for j in range(2):
+            rows = pl.ds(pl.multiple_of(j * 512 + zz * T, T), T)
+            db = dog[zz, :, j * D : (j + 1) * D]
+            do2[rows, :] = db
+            doT[:, rows] = db.T
+
+    @pl.loop(0, SLOTS)
+    def _(d):
+        @pl.when(S >= d)
+        def _():
+            vd = kv[d, 1]
+            scale = jnp.exp2((ms[d, 0:1, :] - st[0:1, :]) * EXP2_SCALE)
+            for c in range(4):
+                cs = slice(c * 256, (c + 1) * 256)
                 dp = dot(vd, doT[:, cs])
-                st[0:1, cs] = top
-                st[1:2, cs] = st[1:2, cs] * keep + jnp.sum(p, axis=0, keepdims=True)
-                st[2:3, cs] = st[2:3, cs] * keep + jnp.sum(p * dp, axis=0, keepdims=True)
-                ms[d, 0:1, cs] = top
-                sbuf[d, :, cs] = p
                 dpbuf[d, :, cs] = dp
-                oT[:, cs] = oT[:, cs] * keep + dot(vt, p.astype(BF16))
+                st[2:3, cs] += scale[:, cs] * jnp.sum(sbuf[d, :, cs] * dp, axis=0, keepdims=True)
 
     stat = remote(st, st_in, st_s, st_r, dev(x, y, wrap(z + 2)))
     stat.start()
@@ -430,24 +455,22 @@
         c.start()
 
     swap[0].wait_recv()
-    final = [[facc[n, pl.ds(erow, T), :], pin[n].astype(F32)] for n in range(2)]
-    for m in (0, 1):
-        chain = (chain8, chain4)[m]
-
+    ggcopies = over_x(gv_o, gvg.at[:, x], gg_s, gg_r)
+    for m, chain in enumerate((chain8, chain4)):
         @pl.when(x < 2 + m)
         def _():
             for c in chain:
                 c.wait_recv()
 
-        for n in range(2):
-            for part in range(2):
-                final[n][part] = final[n][part] + jnp.where(x < 2 + m, cin[m, part, n].astype(F32), 0.0)
     for n, out in ((1, gv_o), (0, gk_o)):
-        out[e] = final[n][0].astype(BF16)
-        out[1 - e] = final[n][1].astype(BF16)
-    ggcopies = over_x(gv_o, gvg.at[:, x], gg_s, gg_r)
-    for c in ggcopies:
-        c.start()
+        parts = [facc[n, pl.ds(erow, T), :], pin[n].astype(F32)]
+        for m in (0, 1):
+            parts = [a + jnp.where(x < 2 + m, cin[m, part, n].astype(F32), 0.0) for part, a in enumerate(parts)]
+        out[e] = parts[0].astype(BF16)
+        out[1 - e] = parts[1].astype(BF16)
+        if n == 1:
+            for c in ggcopies:
+                c.start()
     gvg[:, x] = gv_o[...]
 
     def terms(hh):
@@ -461,19 +484,19 @@
     tb[0] = terms(hzc).astype(BF16)
     far = remote(tb.at[0], hin.at[0], h_s.at[0], h_r.at[0], (i, hc))
     far.start()
-    for c in ggcopies:
-        c.wait_recv()
-    for n in range(2):
-        pv[:, n * D : (n + 1) * D] = dot(winT[0], gvg[n].reshape(4 * T, D)).astype(BF16)
-    yvcopies = over_y(pv, yv, yv_s, yv_r)
-    for c in yvcopies:
-        c.start()
-
     mine_far = terms(hz)
     far.wait_recv()
     tb[1] = (mine_far + hin[0].astype(F32)).astype(BF16)
     across = remote(tb.at[1], hin.at[1], h_s.at[1], h_r.at[1], (i, hz))
     across.start()
+    for c in ggcopies:
+        c.wait_recv()
+    for n in range(2):
+        pv[:, n * D : (n + 1) * D] = dot(winT[0], gvg[n].reshape(4 * T, D)).astype(BF16)
+    yvcopies = over_y(pv, yv, yv_s, yv_r)
+    for c in yvcopies:
+        c.start()
+
     tb[2] = terms(hc).astype(BF16)
     near = remote(tb.at[2], hin.at[2], h_s.at[2], h_r.at[2], (i, hc))
     near.start()

time: 83 us -> 82.5 us (level)
  the two profiles are of different devices: /device:TPU:4 before, /device:TPU:1 now
where the time goes in v4:
time: 82.5 us; the launch traced here: 81.3 us
  Pallas kernels  80.7 us (98%)
    pallas_call x1, Pallas kernels, layer(): pl.pallas_call(layer_kernel, out_shape=(jax.ShapeDtypeStruct((COLS, T), B...  79 us
    pallas_call x1, Pallas kernels, local(): pl.pallas_call(hand_over, out_shape=tuple((jax.ShapeDtypeStruct(a.shape,...  1.68 us

profile of v4, /device:TPU:1, one launch (start us, length us, event | category | flops | bytes accessed | tf_op | source)
XLA Modules:
  0.0 81.3 jit_solution(972542795982068396)
XLA Ops:
  0.6 79.0 %layer.1 = (bf16[576,128]{1,0:T(8,128)(2,1)}, f32[36,256]{1,0:T(8,128)}, f32[36,512]{1,0:T(8,128)}) custom-call(bf16[128,2304]{1,0:T(8,128)(2,1)} %x_hbm.1, bf16[128,512]{1,0:T(8,128)(2,1)} %q_hbm.1, bf16[128,256]{1,0:T(8,128)(2,1)} %k_hbm.1, bf16[128,256]{1,0:T(8,128)(2,1)} %v_hbm.1, bf16[2304,512]{1,0:T(8,128)(2,1)} %wq_hbm.1, bf16[2304,256]{1,0:T(8,128)(2,1)} %wk_hbm.1, ...), custom_call_target="tpu_custom_call" | custom-call | tf_op jit(solution)/shard_map/layer/pallas_call | solution.py:584
  79.6 1.7 %hand_over.1 = (bf16[576,128]{1,0:T(8,128)(2,1)}, f32[36,256]{1,0:T(8,128)}, f32[36,512]{1,0:T(8,128)}) custom-call(bf16[576,128]{1,0:T(8,128)(2,1)} %get-tuple-element.9.refs_0_, f32[36,256]{1,0:T(8,128)} %get-tuple-element.10.refs_1_, f32[36,512]{1,0:T(8,128)} %get-tuple-element.11.refs_2_), custom_call_target="tpu_custom_call" | custom-call | tf_op jit(solution)/shard_map/hand_over/pallas_call | solution.py:669

commit v5 on v4

--- a/solution.py
+++ b/solution.py
@@ -180,6 +180,14 @@
             )
 
     c_q.wait()
+    @pl.when(x >= 2)
+    def _():
+        recv_slot(8)
+        for r in (1, 2, 3):
+            @pl.when(y + r >= 4)
+            def _():
+                fwd_y(r, 1).start()
+
     for c in qcopies:
         c.wait_recv()
 
@@ -191,6 +199,19 @@
             q2[rows, :] = qb
             qT[:, rows] = qb.T
 
+    for c in docopies:
+        c.wait_recv()
+    for c in wcopies + c_win + c_w:
+        c.start()
+
+    @pl.loop(0, 4)
+    def _(zz):
+        for j in range(2):
+            rows = pl.ds(pl.multiple_of(j * 512 + zz * T, T), T)
+            db = dog[zz, :, j * D : (j + 1) * D]
+            do2[rows, :] = db
+            doT[:, rows] = db.T
+
     st[...] = jnp.concatenate([jnp.full((1, ROWS), NEG, F32), jnp.zeros((7, ROWS), F32)], axis=0)
     oT[...] = jnp.zeros_like(oT)
     dqT[...] = jnp.zeros_like(dqT)
@@ -202,7 +223,8 @@
 
     def probabilities(d, edge):
         kd = kv[d, 0]
-        vt = kv[d, 1].T
+        vd = kv[d, 1]
+        vt = vd.T
         low = jnp.where(d == 0, 0, -100000)
         high = jnp.where(d == 8, 0, 100000)
         for c in range(4):
@@ -219,10 +241,13 @@
             top = jnp.maximum(before, jnp.max(s, axis=0, keepdims=True))
             p = jnp.exp2((s - top) * EXP2_SCALE)
             keep = jnp.exp2((before - top) * EXP2_SCALE)
+            dp = dot(vd, doT[:, cs])
             st[0:1, cs] = top
             st[1:2, cs] = st[1:2, cs] * keep + jnp.sum(p, axis=0, keepdims=True)
+            st[2:3, cs] = st[2:3, cs] * keep + jnp.sum(p * dp, axis=0, keepdims=True)
             ms[d, 0:1, cs] = top
             sbuf[d, :, cs] = p
+            dpbuf[d, :, cs] = dp
             oT[:, cs] = oT[:, cs] * keep + dot(vt, p.astype(BF16))
 
     def prob_step(t):
@@ -243,42 +268,7 @@
 
             probabilities(d, False)
 
-    pl.loop(0, 5)(prob_step)
-
-    @pl.when(x >= 2)
-    def _():
-        recv_slot(8)
-        for r in (1, 2, 3):
-            @pl.when(y + r >= 4)
-            def _():
-                fwd_y(r, 1).start()
-
-    pl.loop(5, 12)(prob_step)
-
-    for c in docopies:
-        c.wait_recv()
-    for c in wcopies + c_win + c_w:
-        c.start()
-
-    @pl.loop(0, 4)
-    def _(zz):
-        for j in range(2):
-            rows = pl.ds(pl.multiple_of(j * 512 + zz * T, T), T)
-            db = dog[zz, :, j * D : (j + 1) * D]
-            do2[rows, :] = db
-            doT[:, rows] = db.T
-
-    @pl.loop(0, SLOTS)
-    def _(d):
-        @pl.when(S >= d)
-        def _():
-            vd = kv[d, 1]
-            scale = jnp.exp2((ms[d, 0:1, :] - st[0:1, :]) * EXP2_SCALE)
-            for c in range(4):
-                cs = slice(c * 256, (c + 1) * 256)
-                dp = dot(vd, doT[:, cs])
-                dpbuf[d, :, cs] = dp
-                st[2:3, cs] += scale[:, cs] * jnp.sum(sbuf[d, :, cs] * dp, axis=0, keepdims=True)
+    pl.loop(0, 12)(prob_step)
 
     stat = remote(st, st_in, st_s, st_r, dev(x, y, wrap(z + 2)))
     stat.start()
@@ -341,7 +331,7 @@
                 n = jnp.where(kind, r - 1, r + 2)
                 remote(dkv.at[d], rbuf.at[n], rb_s.at[n], rb_r.at[n], dev(x, wrap(y - r), z)).start()
 
-    pl.loop(0, 8)(grad_step)
+    pl.loop(0, 12)(grad_step)
 
     def recv_back(n):
         remote(rbuf.at[n], rbuf.at[n], rb_s.at[n], rb_r.at[n], dev(x, wrap(y + 1), z)).wait_recv()
@@ -368,8 +358,6 @@
         csend[0] = facc[...].astype(BF16)
         for c in chain8:
             c.start()
-
-    pl.loop(8, 12)(grad_step)
 
     dqcopies = spread(dqT, LOGIT_SCALE, dqsend, dqin, dq_s, dq_r)
 

time: 82.5 us -> 75.1 us (0.910)
  the two profiles are of different devices: /device:TPU:1 before, /device:TPU:13 now
where the time goes in v5:
time: 75.1 us; the launch traced here: 75 us
  Pallas kernels  74.3 us (99%)
    pallas_call x1, Pallas kernels, layer(): pl.pallas_call(layer_kernel, out_shape=(jax.ShapeDtypeStruct((COLS, T), B...  72.6 us
    pallas_call x1, Pallas kernels, local(): pl.pallas_call(hand_over, out_shape=tuple((jax.ShapeDtypeStruct(a.shape,...  1.68 us

profile of v5, /device:TPU:13, one launch (start us, length us, event | category | flops | bytes accessed | tf_op | source)
XLA Modules:
  0.0 75.0 jit_solution(2502172963418928918)
XLA Ops:
  0.6 72.6 %layer.1 = (bf16[576,128]{1,0:T(8,128)(2,1)}, f32[36,256]{1,0:T(8,128)}, f32[36,512]{1,0:T(8,128)}) custom-call(bf16[128,2304]{1,0:T(8,128)(2,1)} %x_hbm.1, bf16[128,512]{1,0:T(8,128)(2,1)} %q_hbm.1, bf16[128,256]{1,0:T(8,128)(2,1)} %k_hbm.1, bf16[128,256]{1,0:T(8,128)(2,1)} %v_hbm.1, bf16[2304,512]{1,0:T(8,128)(2,1)} %wq_hbm.1, bf16[2304,256]{1,0:T(8,128)(2,1)} %wk_hbm.1, ...), custom_call_target="tpu_custom_call" | custom-call | tf_op jit(solution)/shard_map/layer/pallas_call | solution.py:572
  73.3 1.7 %hand_over.1 = (bf16[576,128]{1,0:T(8,128)(2,1)}, f32[36,256]{1,0:T(8,128)}, f32[36,512]{1,0:T(8,128)}) custom-call(bf16[576,128]{1,0:T(8,128)(2,1)} %get-tuple-element.9.refs_0_, f32[36,256]{1,0:T(8,128)} %get-tuple-element.10.refs_1_, f32[36,512]{1,0:T(8,128)} %get-tuple-element.11.refs_2_), custom_call_target="tpu_custom_call" | custom-call | tf_op jit(solution)/shard_map/hand_over/pallas_call | solution.py:657
